TPU v7x, 32 devices: a whole 2x2x4 slice. The times are simulated.
32 devices in a mesh: dp: 8 (over z, x), tensor: 4 (over y, core).
Axes of the slice: x: 2, y: 2, z: 4, core: 2. Of those that a mesh axis runs over, the one named last changes fastest.
Arguments:
- tokens: bfloat16 [128, 64, 768], P('dp'), may hold values from -6 to 6
- image_tokens: bfloat16 [128, 256, 768], P('dp', None, 'tensor'), may hold values from -6 to 6
- image_counts: int32 [128], P('dp'), may hold values from 64 to 256, as said below
- ln1_gain: float32 [768], replicated, may hold values from 0.25 to 1.75
- ln1_bias: float32 [768], replicated, may hold values from -2 to 2
- self_qkv: bfloat16 [768, 3, 768], P(None, None, 'tensor'), may hold values from -0.21875 to 0.21875
- self_output_weight: bfloat16 [768, 768], P('tensor'), may hold values from -0.625 to 0.625
- self_output_bias: float32 [768], replicated, may hold values from -2 to 2
- ln2_gain: float32 [768], replicated, may hold values from 0.25 to 1.75
- ln2_bias: float32 [768], replicated, may hold values from -2 to 2
- cross_query_weight: bfloat16 [768, 768], P(None, 'tensor'), may hold values from -0.21875 to 0.21875
- cross_kv: bfloat16 [768, 2, 768], P(None, None, 'tensor'), may hold values from -0.21875 to 0.21875
- cross_output_weight: bfloat16 [768, 768], P('tensor'), may hold values from -0.625 to 0.625
- cross_output_bias: float32 [768], replicated, may hold values from -2 to 2
- ln3_gain: float32 [768], replicated, may hold values from 0.25 to 1.75
- ln3_bias: float32 [768], replicated, may hold values from -2 to 2
- mlp_in: bfloat16 [768, 3072], P(None, 'tensor'), may hold values from -0.21875 to 0.21875
- mlp_in_bias: float32 [3072], P('tensor'), may hold values from -3 to 3
- mlp_out: bfloat16 [3072, 768], P('tensor'), may hold values from -0.15625 to 0.15625
- mlp_out_bias: float32 [768], replicated, may hold values from -2 to 2
- grad_out: bfloat16 [128, 64, 768], P('dp'), may hold values from -6 to 6
Outputs:
- output: bfloat16 [128, 64, 768], P('dp')
- grad_tokens: bfloat16 [128, 64, 768], P('dp')
- grad_image: bfloat16 [128, 256, 768], P('dp', None, 'tensor')
- grad_ln1_gain: float32 [768], replicated
- grad_ln1_bias: float32 [768], replicated
- grad_self_qkv: float32 [768, 3, 768], P('dp', None, 'tensor')
- grad_self_out: float32 [768, 768], P('tensor', 'dp')
- grad_self_out_bias: float32 [768], replicated
- grad_ln2_gain: float32 [768], replicated
- grad_ln2_bias: float32 [768], replicated
- grad_cross_q: float32 [768, 768], P('dp', 'tensor')
- grad_cross_kv: float32 [768, 2, 768], P('dp', None, 'tensor')
- grad_cross_out: float32 [768, 768], P('tensor', 'dp')
- grad_cross_out_bias: float32 [768], replicated
- grad_ln3_gain: float32 [768], replicated
- grad_ln3_bias: float32 [768], replicated
- grad_mlp_in: float32 [768, 3072], P('dp', 'tensor')
- grad_mlp_in_bias: float32 [3072], P('tensor')
- grad_mlp_out: float32 [3072, 768], P('tensor', 'dp')
- grad_mlp_out_bias: float32 [768], replicated
Inputs may be any that keep to these rules, and one draw needn't show every extreme that they name: image_counts[c] is the number of leading image tokens that caption c attends to; both bounds are reached in every draw.
All inputs are finite; a program needn't handle non-finite values.
Results may differ from a plain program's by a relative error of at most 0.034.
Values may be sent and summed in bfloat16 or wider, within the bound.
A program may use at most 192 MiB of HBM per device.

v0:
```python
from functools import partial

import jax
import jax.numpy as jnp
from jax import lax
from jax.sharding import PartitionSpec as P

HEAD_SIZE = 64


def norm_parts(values):
    center = values - jnp.mean(values, axis=-1, keepdims=True)
    inv_std = lax.rsqrt(jnp.mean(center * center, axis=-1, keepdims=True) + 1e-05)
    return (center * inv_std, inv_std)


def norm_back(gradient, normed, inv_std, gain_row):
    scaled = gradient * gain_row
    return inv_std * (
        scaled
        - jnp.mean(scaled, axis=-1, keepdims=True)
        - normed * jnp.mean(scaled * normed, axis=-1, keepdims=True)
    )


def branch_total(term_rows):
    return lax.psum(term_rows.astype(jnp.bfloat16), "tensor").astype(jnp.float32)


def input_total(term_rows):
    return lax.psum(term_rows.astype(jnp.bfloat16), "tensor").astype(jnp.float32)


def attend_forward(queries, key_rows, value_rows, allowed, scaling):
    scores = (
        jnp.einsum("clhe,cmhe->chlm", queries, key_rows, preferred_element_type=jnp.float32)
        * scaling
    )
    scores = jnp.where(allowed[:, None], scores, -1000000000.0)
    highest = jnp.max(scores, axis=-1, keepdims=True)
    exponent = jnp.exp(scores - highest)
    chances = exponent / jnp.sum(exponent, axis=-1, keepdims=True)
    mixture = jnp.einsum(
        "chlm,cmhe->clhe",
        chances.astype(jnp.bfloat16),
        value_rows,
        preferred_element_type=jnp.float32,
    )
    return (mixture.astype(jnp.bfloat16), chances)


def attend_back(grad_mixture, queries, key_rows, value_rows, chances, scaling):
    grad_chances = jnp.einsum(
        "clhe,cmhe->chlm", grad_mixture, value_rows, preferred_element_type=jnp.float32
    )
    grad_values = jnp.einsum(
        "chlm,clhe->cmhe",
        chances.astype(jnp.bfloat16),
        grad_mixture,
        preferred_element_type=jnp.float32,
    )
    inner_sum = jnp.sum(grad_chances * chances, axis=-1, keepdims=True)
    grad_scores = (chances * (grad_chances - inner_sum)).astype(jnp.bfloat16)
    grad_queries = (
        jnp.einsum("chlm,cmhe->clhe", grad_scores, key_rows, preferred_element_type=jnp.float32)
        * scaling
    )
    grad_keys = (
        jnp.einsum("chlm,clhe->cmhe", grad_scores, queries, preferred_element_type=jnp.float32)
        * scaling
    )
    return (
        grad_queries.astype(jnp.bfloat16),
        grad_keys.astype(jnp.bfloat16),
        grad_values.astype(jnp.bfloat16),
    )


def local(
    tokens,
    image_tokens,
    image_counts,
    ln1_gain,
    ln1_bias,
    self_qkv,
    self_output_weight,
    self_output_bias,
    ln2_gain,
    ln2_bias,
    cross_query_weight,
    cross_kv,
    cross_output_weight,
    cross_output_bias,
    ln3_gain,
    ln3_bias,
    mlp_in,
    mlp_in_bias,
    mlp_out,
    mlp_out_bias,
    grad_out,
):
    captions, length, model_width = tokens.shape
    row_count = captions * length
    local_width = self_output_weight.shape[0]
    local_heads = local_width // HEAD_SIZE
    scaling = HEAD_SIZE ** (-0.5)
    residual = tokens.astype(jnp.float32).reshape(row_count, model_width)
    normed_one, inv_one = norm_parts(residual)
    in_one = (normed_one * ln1_gain + ln1_bias).astype(jnp.bfloat16)
    qkv_rows = jnp.einsum(
        "rd,dtk->rtk", in_one, self_qkv, preferred_element_type=jnp.float32
    ).astype(jnp.bfloat16)
    qkv_view = qkv_rows.reshape(captions, length, 3, local_heads, HEAD_SIZE)
    queries_one, keys_one, values_one = (qkv_view[:, :, 0], qkv_view[:, :, 1], qkv_view[:, :, 2])
    positions = jnp.arange(length)
    causal = jnp.broadcast_to(positions[:, None] >= positions[None, :], (captions, length, length))
    mixture_one, chances_one = attend_forward(queries_one, keys_one, values_one, causal, scaling)
    mixture_one = mixture_one.reshape(row_count, local_width)
    after_first_residual = (
        residual
        + branch_total(jnp.dot(mixture_one, self_output_weight, preferred_element_type=jnp.float32))
        + self_output_bias
    )
    second_normalized, inv_two = norm_parts(after_first_residual)
    in_two = (second_normalized * ln2_gain + ln2_bias).astype(jnp.bfloat16)
    second_query_rows = (
        jnp.dot(in_two, cross_query_weight, preferred_element_type=jnp.float32)
        .astype(jnp.bfloat16)
        .reshape(captions, length, local_heads, HEAD_SIZE)
    )
    image_full = lax.all_gather(image_tokens, "tensor", axis=2, tiled=True)
    image_count = image_full.shape[1]
    kv_rows = jnp.einsum(
        "cid,dtk->citk", image_full, cross_kv, preferred_element_type=jnp.float32
    ).astype(jnp.bfloat16)
    kv_view = kv_rows.reshape(captions, image_count, 2, local_heads, HEAD_SIZE)
    keys_two, values_two = (kv_view[:, :, 0], kv_view[:, :, 1])
    valid_keys = jnp.arange(image_count)[None, :] < image_counts[:, None]
    cross_mask = jnp.broadcast_to(valid_keys[:, None, :], (captions, length, image_count))
    mixture_two, chances_two = attend_forward(
        second_query_rows, keys_two, values_two, cross_mask, scaling
    )
    mixture_two = mixture_two.reshape(row_count, local_width)
    after_second_residual = (
        after_first_residual
        + branch_total(
            jnp.dot(mixture_two, cross_output_weight, preferred_element_type=jnp.float32)
        )
        + cross_output_bias
    )
    normed_three, inv_three = norm_parts(after_second_residual)
    in_three = (normed_three * ln3_gain + ln3_bias).astype(jnp.bfloat16)
    pre_act = jnp.dot(in_three, mlp_in, preferred_element_type=jnp.float32) + mlp_in_bias
    activated, gelu_pull = jax.vjp(partial(jax.nn.gelu, approximate=False), pre_act)
    act_low = activated.astype(jnp.bfloat16)
    result = (
        after_second_residual
        + branch_total(jnp.dot(act_low, mlp_out, preferred_element_type=jnp.float32))
        + mlp_out_bias
    )
    output = result.astype(jnp.bfloat16).reshape(tokens.shape)
    grad_rows = grad_out.astype(jnp.float32).reshape(row_count, model_width)
    grad_low = grad_rows.astype(jnp.bfloat16)
    grad_mlp_out_local = jnp.einsum(
        "rf,rd->fd", act_low, grad_low, preferred_element_type=jnp.float32
    )
    grad_hidden = jnp.einsum("rd,fd->rf", grad_low, mlp_out, preferred_element_type=jnp.float32)
    (grad_pre,) = gelu_pull(grad_hidden)
    grad_pre_low = grad_pre.astype(jnp.bfloat16)
    grad_mlp_in_bias = jnp.sum(grad_pre_low, axis=0, dtype=jnp.float32)
    grad_mlp_in_local = jnp.einsum(
        "rd,rf->df", in_three, grad_pre_low, preferred_element_type=jnp.float32
    )
    grad_in_three = input_total(
        jnp.einsum("rf,df->rd", grad_pre_low, mlp_in, preferred_element_type=jnp.float32)
    )
    grad_gain_three = jnp.sum(grad_in_three * normed_three, axis=0)
    grad_bias_three = jnp.sum(grad_in_three, axis=0)
    grad_two = grad_rows + norm_back(grad_in_three, normed_three, inv_three, ln3_gain)
    grad_two_low = grad_two.astype(jnp.bfloat16)
    grad_cross_bias = jnp.sum(grad_two, axis=0)
    grad_cross_out_local = jnp.einsum(
        "rk,rd->kd", mixture_two, grad_two_low, preferred_element_type=jnp.float32
    )
    grad_mix_two = jnp.einsum(
        "rd,kd->rk", grad_two_low, cross_output_weight, preferred_element_type=jnp.float32
    ).astype(jnp.bfloat16)
    grad_mix_two = grad_mix_two.reshape(captions, length, local_heads, HEAD_SIZE)
    grad_query_two, grad_keys_two, grad_values_two = attend_back(
        grad_mix_two, second_query_rows, keys_two, values_two, chances_two, scaling
    )
    grad_kv = jnp.stack([grad_keys_two, grad_values_two], axis=2).reshape(
        captions, image_count, 2, local_width
    )
    grad_cross_kv_local = jnp.einsum(
        "cid,citk->dtk", image_full, grad_kv, preferred_element_type=jnp.float32
    )
    image_terms = jnp.einsum("citk,dtk->cid", grad_kv, cross_kv, preferred_element_type=jnp.float32)
    grad_image = lax.psum_scatter(
        image_terms.astype(jnp.bfloat16), "tensor", scatter_dimension=2, tiled=True
    )
    query_rows_two = grad_query_two.reshape(row_count, local_width)
    grad_cross_q_local = jnp.einsum(
        "rd,rk->dk", in_two, query_rows_two, preferred_element_type=jnp.float32
    )
    grad_in_two = input_total(
        jnp.einsum(
            "rk,dk->rd", query_rows_two, cross_query_weight, preferred_element_type=jnp.float32
        )
    )
    grad_gain_two = jnp.sum(grad_in_two * second_normalized, axis=0)
    grad_bias_two = jnp.sum(grad_in_two, axis=0)
    grad_one = grad_two + norm_back(grad_in_two, second_normalized, inv_two, ln2_gain)
    grad_one_low = grad_one.astype(jnp.bfloat16)
    grad_self_bias = jnp.sum(grad_one, axis=0)
    grad_self_out_local = jnp.einsum(
        "rk,rd->kd", mixture_one, grad_one_low, preferred_element_type=jnp.float32
    )
    grad_mix_one = jnp.einsum(
        "rd,kd->rk", grad_one_low, self_output_weight, preferred_element_type=jnp.float32
    ).astype(jnp.bfloat16)
    grad_mix_one = grad_mix_one.reshape(captions, length, local_heads, HEAD_SIZE)
    grad_query_one, grad_keys_one, grad_values_one = attend_back(
        grad_mix_one, queries_one, keys_one, values_one, chances_one, scaling
    )
    grad_qkv = jnp.stack([grad_query_one, grad_keys_one, grad_values_one], axis=2).reshape(
        row_count, 3, local_width
    )
    grad_self_qkv_local = jnp.einsum(
        "rd,rtk->dtk", in_one, grad_qkv, preferred_element_type=jnp.float32
    )
    grad_in_one = input_total(
        jnp.einsum("rtk,dtk->rd", grad_qkv, self_qkv, preferred_element_type=jnp.float32)
    )
    grad_gain_one = jnp.sum(grad_in_one * normed_one, axis=0)
    grad_bias_one = jnp.sum(grad_in_one, axis=0)
    grad_tokens = (
        (grad_one + norm_back(grad_in_one, normed_one, inv_one, ln1_gain))
        .astype(jnp.bfloat16)
        .reshape(tokens.shape)
    )
    grad_out_bias = jnp.sum(grad_rows, axis=0)
    (
        grad_self_qkv,
        grad_self_out,
        grad_cross_q,
        grad_cross_kv,
        grad_cross_out,
        grad_mlp_in,
        grad_mlp_out,
    ) = (
        lax.psum_scatter(grad_self_qkv_local, "dp", scatter_dimension=0, tiled=True),
        lax.psum_scatter(grad_self_out_local, "dp", scatter_dimension=1, tiled=True),
        lax.psum_scatter(grad_cross_q_local, "dp", scatter_dimension=0, tiled=True),
        lax.psum_scatter(grad_cross_kv_local, "dp", scatter_dimension=0, tiled=True),
        lax.psum_scatter(grad_cross_out_local, "dp", scatter_dimension=1, tiled=True),
        lax.psum_scatter(grad_mlp_in_local, "dp", scatter_dimension=0, tiled=True),
        lax.psum_scatter(grad_mlp_out_local, "dp", scatter_dimension=1, tiled=True),
    )
    (
        grad_gain_one,
        grad_bias_one,
        grad_self_bias,
        grad_gain_two,
        grad_bias_two,
        grad_cross_bias,
        grad_gain_three,
        grad_bias_three,
        grad_mlp_in_bias,
        grad_out_bias,
    ) = lax.psum(
        (
            grad_gain_one,
            grad_bias_one,
            grad_self_bias,
            grad_gain_two,
            grad_bias_two,
            grad_cross_bias,
            grad_gain_three,
            grad_bias_three,
            grad_mlp_in_bias,
            grad_out_bias,
        ),
        "dp",
    )
    return (
        output,
        grad_tokens,
        grad_image,
        grad_gain_one,
        grad_bias_one,
        grad_self_qkv,
        grad_self_out,
        grad_self_bias,
        grad_gain_two,
        grad_bias_two,
        grad_cross_q,
        grad_cross_kv,
        grad_cross_out,
        grad_cross_bias,
        grad_gain_three,
        grad_bias_three,
        grad_mlp_in,
        grad_mlp_in_bias,
        grad_mlp_out,
        grad_out_bias,
    )


def solution(mesh):
    return jax.shard_map(
        local,
        mesh=mesh,
        in_specs=(
            P("dp", None, None),
            P("dp", None, "tensor"),
            P("dp"),
            P(),
            P(),
            P(None, None, "tensor"),
            P("tensor", None),
            P(),
            P(),
            P(),
            P(None, "tensor"),
            P(None, None, "tensor"),
            P("tensor", None),
            P(),
            P(),
            P(),
            P(None, "tensor"),
            P("tensor"),
            P("tensor", None),
            P(),
            P("dp", None, None),
        ),
        out_specs=(
            P("dp", None, None),
            P("dp", None, None),
            P("dp", None, "tensor"),
            P(),
            P(),
            P("dp", None, "tensor"),
            P("tensor", "dp"),
            P(),
            P(),
            P(),
            P("dp", "tensor"),
            P("dp", None, "tensor"),
            P("tensor", "dp"),
            P(),
            P(),
            P(),
            P("dp", "tensor"),
            P("tensor"),
            P("tensor", "dp"),
            P(),
        ),
        check_vma=False,
    )
```

profile of v0, /device:TPU:0, one launch (start us, length us, event | category | flops | bytes accessed | tf_op | source)
XLA Modules:
  0.0 956.3 jit_solution(9521117675636398474)
XLA Ops:
  14.8 4.2 reshape.186
  31.6 3.6 fusion.59
  44.7 44.1 %all-reduce.8.cloned.1.call-done = bf16[1024,768]{1,0:T(8,128)(2,1)} async-done(((bf16[1024,768]{1,0:T(8,128)(2,1)}), bf16[1024,768]{1,0:T(8,128)(2,1)}) %all-reduce.8.cloned.1.call-update) | async-done | bytes 1572880 | tf_op jit(solution)/shard_map/psum | solution.py:27
  97.8 39.0 %all-gather.2.cloned.1.call-done = bf16[16,256,768]{1,2,0:T(8,128)(2,1)} async-done(((bf16[16,256,192]{1,2,0:T(8,128)(2,1)}), bf16[16,256,768]{1,2,0:T(8,128)(2,1)}) %all-gather.2.cloned.1.call-update) | async-done | bytes 6291472 | tf_op jit(solution)/shard_map/all_gather | solution.py:131
  136.8 5.6 fusion.46
  157.7 40.0 %all-reduce.10.cloned.1.call-done = bf16[1024,768]{1,0:T(8,128)(2,1)} async-done(((bf16[1024,768]{1,0:T(8,128)(2,1)}), bf16[1024,768]{1,0:T(8,128)(2,1)}) %all-reduce.10.cloned.1.call-update) | async-done | bytes 1572880 | tf_op jit(solution)/shard_map/psum | solution.py:27
  204.9 10.3 %convert_reduce_fusion.5 = (f32[768]{0:T(1024)}, bf16[1024,768]{1,0:T(8,128)(2,1)S(1)}, f32[1024,768]{1,0:T(8,128)}) fusion(f32[1024,768]{1,0:T(8,128)S(1)} %fusion.100, f32[768]{0:T(1024)S(1)} %copy-done.59, bf16[1024,768]{1,0:T(8,128)(2,1)S(1)} %copy-done.29, bf16[768,768]{1,0:T(8,128)(2,1)S(1)} %copy-done), kind=kOutput, calls=%fused_computation.59 | convolution fusion | flops 1266941184 | bytes 10622976 | tf_op jit(solution)/shard_map/rd,fd->rf/dot_general | solution.py:167
  219.3 4.4 multiply_convert_fusion.2
  223.7 38.3 %all-reduce.12.cloned.1.call-done = bf16[1024,768]{1,0:T(8,128)(2,1)} async-done(((bf16[1024,768]{1,0:T(8,128)(2,1)}), bf16[1024,768]{1,0:T(8,128)(2,1)}) %all-reduce.12.cloned.1.call-update) | async-done | bytes 1572880 | tf_op jit(solution)/shard_map/psum | solution.py:31
  262.0 4.4 fusion.29
  275.1 4.0 multiply_reduce_fusion
  290.8 4.1 convolution_convert_fusion.3
  299.2 11.6 %reduce-scatter.25.cloned.1.call-start = ((), (), s32[]{:S(2)}) async-start(), calls=%async_computation.18 | async-start | bytes 884736
  310.8 23.0 %all-reduce.14.cloned.1.call-done = bf16[1024,768]{1,0:T(8,128)(2,1)} async-done(((bf16[1024,768]{1,0:T(8,128)(2,1)}), bf16[1024,768]{1,0:T(8,128)(2,1)}) %all-reduce.14.cloned.1.call-update) | async-done | bytes 1572880 | tf_op jit(solution)/shard_map/psum | solution.py:31
  333.8 4.2 fusion.30
  347.7 7.1 fusion.2
  363.3 3.7 fusion.60
  391.8 3.8 bitcast_convert_fusion.1
  399.5 4.8 fusion.103
  404.6 4.7 fusion.102
  409.4 4.7 fusion.50
  414.1 7.4 bitcast_convert_fusion
  425.1 40.9 %reduce-scatter.25.cloned.1.call-done = f32[96,192]{1,0:T(8,128)} async-done(((f32[768,192]{1,0:T(8,128)}), f32[96,192]{1,0:T(8,128)}) %reduce-scatter.25.cloned.1.call-update) | async-done | bytes 73744
  467.6 65.5 %reduce-scatter.27.cloned.1.call-done = f32[96,384]{1,0:T(8,128)} async-done(((f32[768,384]{1,0:T(8,128)}), f32[96,384]{1,0:T(8,128)}) %reduce-scatter.27.cloned.1.call-update) | async-done | bytes 147472
  535.0 68.7 %all-reduce.16.cloned.1.call-done = (bf16[1024,768]{1,0:T(8,128)(2,1)}, bf16[1024,768]{1,0:T(8,128)(2,1)}) async-done(((bf16[1024,768]{1,0:T(8,128)(2,1)}, bf16[1024,768]{1,0:T(8,128)(2,1)}), (bf16[1024,768]{1,0:T(8,128)(2,1)}, bf16[1024,768]{1,0:T(8,128)(2,1)})) %all-reduce.16.cloned.1.call-update) | async-done | bytes 3145744 | tf_op jit(solution)/shard_map/psum | solution.py:27
  606.6 38.2 %all-reduce = (f32[768]{0:T(1024)}, f32[768]{0:T(1024)}, f32[768]{0:T(1024)}, f32[768]{0:T(1024)}, f32[768]{0:T(1024)}, /*index=5*/f32[768]{0:T(1024)}, f32[768]...) all-reduce(f32[768]{0:T(1024)S(1)} %get-tuple-element.84, ...), channel_id=1, replica_groups=mesh['dp'=8,'tensor'=4] {'dp'}, use_global_device_ids=true, to_apply=%region_26.27 | all-reduce | flops 7680 | bytes 61440 | tf_op jit(solution)/shard_map/psum | solution.py:271
  644.8 4.1 add_convert_fusion.1
  651.1 19.6 %reduce-scatter.19.cloned.1.call-done = f32[96,192]{1,0:T(8,128)} async-done(((f32[768,192]{1,0:T(8,128)}), f32[96,192]{1,0:T(8,128)}) %reduce-scatter.19.cloned.1.call-update) | async-done | bytes 73744 | tf_op jit(solution)/shard_map/reduce_scatter | solution.py:254
  670.7 73.0 %reduce-scatter.23.cloned.1.call-done = f32[768,96]{0,1:T(8,128)} async-done(((f32[768,768]{0,1:T(8,128)}), f32[768,96]{0,1:T(8,128)}) %reduce-scatter.23.cloned.1.call-update) | async-done | bytes 294928 | tf_op jit(solution)/shard_map/reduce_scatter | solution.py:258
  743.7 72.7 %reduce-scatter.21.cloned.1.call-done = f32[96,768]{1,0:T(8,128)} async-done(((f32[768,768]{1,0:T(8,128)}), f32[96,768]{1,0:T(8,128)}) %reduce-scatter.21.cloned.1.call-update) | async-done | bytes 294928 | tf_op jit(solution)/shard_map/reduce_scatter | solution.py:257
  816.4 73.0 %reduce-scatter.17.cloned.1.call-done = f32[96,3,192]{2,0,1:T(8,128)} async-done(((f32[768,3,192]{2,0,1:T(8,128)}), f32[96,3,192]{2,0,1:T(8,128)}) %reduce-scatter.17.cloned.1.call-update) | async-done | bytes 221200 | tf_op jit(solution)/shard_map/reduce_scatter | solution.py:252
  889.3 60.2 %reduce-scatter.15.cloned.1.call-done = bf16[16,256,192]{1,2,0:T(8,128)(2,1)} async-done(((bf16[16,256,768]{1,2,0:T(8,128)(2,1)}), bf16[16,256,192]{1,2,0:T(8,128)(2,1)}) %reduce-scatter.15.cloned.1.call-update) | async-done | bytes 1572880 | tf_op jit(solution)/shard_map/reduce_scatter | solution.py:199
  (256 shorter events, 148.6 us)
Async XLA Ops:
  7.2 197.1 %copy-start = (bf16[768,768]{1,0:T(8,128)(2,1)S(1)}, bf16[768,768]{1,0:T(8,128)(2,1)}, u32[]{:S(2)}) copy-start(bf16[768,768]{1,0:T(8,128)(2,1)} %param.39) | copy-start | bytes 3538948
  7.2 81.6 %all-reduce.8.cloned.1.call-start = ((), (), s32[]{:S(2)}) async-start(), calls=%async_computation.8 | async-start | bytes 3145728 | tf_op jit(solution)/shard_map/psum | solution.py:27
  37.8 6.3 copy-start.67
  37.8 51.0 %copy-start.36 = (f32[768]{0:T(1024)S(1)}, f32[768]{0:T(1024)}, u32[]{:S(2)}) copy-start(f32[768]{0:T(1024)} %param.28) | copy-start | bytes 9220
  43.1 93.8 %all-gather.2.cloned.1.call-start = ((), (), s32[]{:S(2)}) async-start(), calls=%async_computation.9 | async-start | bytes 7864320 | tf_op jit(solution)/shard_map/all_gather | solution.py:131
  43.8 153.9 %all-reduce.10.cloned.1.call-start = ((), (), s32[]{:S(2)}) async-start(), calls=%async_computation.10 | async-start | bytes 3145728 | tf_op jit(solution)/shard_map/psum | solution.py:27
  136.8 5.6 copy-start.14
  151.8 45.9 %copy-start.61 = (f32[768]{0:T(1024)S(1)}, f32[768]{0:T(1024)}, u32[]{:S(2)}) copy-start(f32[768]{0:T(1024)} %param.34) | copy-start | bytes 9220
  154.7 107.3 %all-reduce.12.cloned.1.call-start = ((), (), s32[]{:S(2)}) async-start(), calls=%async_computation.11 | async-start | bytes 3145728 | tf_op jit(solution)/shard_map/psum | solution.py:31
  204.9 10.3 %copy-start.25 = (f32[1024,768]{1,0:T(8,128)}, f32[1024,768]{1,0:T(8,128)S(1)}, u32[]{:S(2)}) copy-start(f32[1024,768]{1,0:T(8,128)S(1)} %fusion.100) | copy-start | bytes 9437188
  218.9 114.9 %all-reduce.14.cloned.1.call-start = ((), (), s32[]{:S(2)}) async-start(), calls=%async_computation.12 | async-start | bytes 3145728 | tf_op jit(solution)/shard_map/psum | solution.py:31
  290.7 132.7 %reduce-scatter.29.cloned.1.call-start = ((), (), s32[]{:S(2)}) async-start(), calls=%async_computation.20 | async-start | bytes 884736
  297.5 36.3 %copy-start.42 = (f32[1024]{0:T(1024)S(1)}, f32[1024]{0:T(1024)}, u32[]{:S(2)}) copy-start(f32[1024]{0:T(1024)} %copy-done.41) | copy-start | bytes 12292
  299.2 166.8 %reduce-scatter.25.cloned.1.call-start = ((), (), s32[]{:S(2)}) async-start(), calls=%async_computation.18 | async-start | bytes 884736
  344.8 188.3 %reduce-scatter.27.cloned.1.call-start = ((), (), s32[]{:S(2)}) async-start(), calls=%async_computation.19 | async-start | bytes 1327104
  347.7 7.1 copy-start.71
  357.5 246.1 %all-reduce.16.cloned.1.call-start = ((), (), s32[]{:S(2)}) async-start(), calls=%async_computation.21 | async-start | bytes 6291456 | tf_op jit(solution)/shard_map/psum | solution.py:27
  395.5 275.1 %reduce-scatter.19.cloned.1.call-start = ((), (), s32[]{:S(2)}) async-start(), calls=%async_computation.15 | async-start | bytes 884736 | tf_op jit(solution)/shard_map/reduce_scatter | solution.py:254
  399.4 344.2 %reduce-scatter.23.cloned.1.call-start = ((), (), s32[]{:S(2)}) async-start(), calls=%async_computation.17 | async-start | bytes 2654208 | tf_op jit(solution)/shard_map/reduce_scatter | solution.py:258
  404.3 412.1 %reduce-scatter.21.cloned.1.call-start = ((), (), s32[]{:S(2)}) async-start(), calls=%async_computation.16 | async-start | bytes 2654208 | tf_op jit(solution)/shard_map/reduce_scatter | solution.py:257
  409.3 480.0 %reduce-scatter.17.cloned.1.call-start = ((), (), s32[]{:S(2)}) async-start(), calls=%async_computation.14 | async-start | bytes 2654208 | tf_op jit(solution)/shard_map/reduce_scatter | solution.py:252
  414.1 535.5 %reduce-scatter.15.cloned.1.call-start = ((), (), s32[]{:S(2)}) async-start(), calls=%async_computation.13 | async-start | bytes 7864320 | tf_op jit(solution)/shard_map/reduce_scatter | solution.py:199
  421.5 182.1 %copy-start.40 = (f32[1024]{0:T(1024)S(1)}, f32[1024]{0:T(1024)}, u32[]{:S(2)}) copy-start(f32[1024]{0:T(1024)} %copy-done.39) | copy-start | bytes 12292
  421.5 182.1 %copy-start.46 = (f32[768]{0:T(1024)S(1)}, f32[768]{0:T(1024)}, u32[]{:S(2)}) copy-start(f32[768]{0:T(1024)} %param.24) | copy-start | bytes 9220
  421.6 185.0 %copy-start.53 = (f32[768]{0:T(1024)S(1)}, f32[768]{0:T(1024)}, u32[]{:S(2)}) copy-start(f32[768]{0:T(1024)} %get-tuple-element.107) | copy-start | bytes 9220
  421.6 185.0 %copy-start.54 = (f32[768]{0:T(1024)S(1)}, f32[768]{0:T(1024)}, u32[]{:S(2)}) copy-start(f32[768]{0:T(1024)} %get-tuple-element.80) | copy-start | bytes 9220
  421.6 185.0 %copy-start.55 = (f32[768]{0:T(1024)S(1)}, f32[768]{0:T(1024)}, u32[]{:S(2)}) copy-start(f32[768]{0:T(1024)} %get-tuple-element.90) | copy-start | bytes 9220
  421.6 185.0 %copy-start.56 = (f32[768]{0:T(1024)S(1)}, f32[768]{0:T(1024)}, u32[]{:S(2)}) copy-start(f32[768]{0:T(1024)} %get-tuple-element.109) | copy-start | bytes 9220
  421.6 185.0 %copy-start.57 = (f32[768]{0:T(1024)S(1)}, f32[768]{0:T(1024)}, u32[]{:S(2)}) copy-start(f32[768]{0:T(1024)} %get-tuple-element.82) | copy-start | bytes 9220
  421.6 185.0 %copy-start.58 = (f32[768]{0:T(1024)S(1)}, f32[768]{0:T(1024)}, u32[]{:S(2)}) copy-start(f32[768]{0:T(1024)} %get-tuple-element.89) | copy-start | bytes 9220
  421.6 185.0 %copy-start.63 = (f32[768]{0:T(1024)S(1)}, f32[768]{0:T(1024)}, u32[]{:S(2)}) copy-start(f32[768]{0:T(1024)} %get-tuple-element.104) | copy-start | bytes 9220
  421.6 223.2 %copy-start.66 = (f32[768]{0:T(1024)S(1)}, f32[768]{0:T(1024)}, u32[]{:S(2)}) copy-start(f32[768]{0:T(1024)} %param.40) | copy-start | bytes 9220
  (55 other events, 148.4 us)
Sparse Core Ops, SparseCore 0:
  43.2 45.5 all-reduce.7
  90.4 46.4 all-gather.1
  154.8 42.8 all-reduce.9
  219.1 42.8 all-reduce.11
  290.9 42.9 all-reduce.13
  337.0 63.3 reduce-scatter.28
  403.6 62.2 reduce-scatter.24
  469.4 63.7 reduce-scatter.26
  536.1 67.4 all-reduce.15
  607.4 63.2 reduce-scatter.18
  674.7 68.8 reduce-scatter.22
  747.6 68.7 reduce-scatter.20
  820.4 68.8 reduce-scatter.16
  892.3 57.2 reduce-scatter.14
where the time goes:
time: 964 us; the launch traced here: 956 us
  waiting for transfers between devices  659 us (68%)
  matrix products  105 us (11%)
  local copies, waits for them, and re-layouts  71.6 us (7%)
  other arithmetic  54.1 us (6%)
  blocking collectives  38.2 us (4%)
  between operations  15 us (2%)
  starting transfers between devices  13.1 us (1%)
    psum x3, waiting for transfers between devices, branch_total(): lax.psum(term_rows.astype(jnp.bfloat16), 'tensor').astype(jnp.float32)  153 us
    unnamed x17, waiting for transfers between devices  107 us
    reduce_scatter x1, waiting for transfers between devices, local(): lax.psum_scatter(grad_mlp_out_local, 'dp', scatter_dimension=1, tiled=True)  73 us
    reduce_scatter x1, waiting for transfers between devices, local(): lax.psum_scatter(grad_self_qkv_local, 'dp', scatter_dimension=0, tiled=True)  73 us
    reduce_scatter x1, waiting for transfers between devices, local(): lax.psum_scatter(grad_mlp_in_local, 'dp', scatter_dimension=0, tiled=True)  72.7 us
    psum x2, waiting for transfers between devices, input_total(): lax.psum(term_rows.astype(jnp.bfloat16), 'tensor').astype(jnp.float32)  61.2 us
    reduce_scatter x1, waiting for transfers between devices, local(): lax.psum_scatter(image_terms.astype(jnp.bfloat16), 'tensor', scatter_dime...  60.2 us
    all_gather x1, waiting for transfers between devices, local(): image_full = lax.all_gather(image_tokens, 'tensor', axis=2, tiled=True)  39 us
  transfers between devices with their start and end apart: 14, of which 13 were waited for; matrix products, arithmetic and copies ran while one was open for 13% of the time, Pallas kernels for 0%

commit v1 on v0

v1 whole, which is shorter than its diff:
```python
from functools import partial

import jax
import jax.numpy as jnp
from jax import lax
from jax.experimental import pallas as pl
from jax.experimental.pallas import tpu as pltpu
from jax.sharding import PartitionSpec as P

HEAD_SIZE = 64
LOW = jnp.bfloat16
HIGH = jnp.float32
MESH = pl.DeviceIdType.MESH
SCALING = HEAD_SIZE**-0.5


def dot(left, right):
    return jnp.dot(left, right, preferred_element_type=HIGH)


def dot_rows(left, right):
    return lax.dot_general(left, right, (((1,), (1,)), ((), ())), preferred_element_type=HIGH)


def dot_columns(left, right):
    return lax.dot_general(left, right, (((0,), (0,)), ((), ())), preferred_element_type=HIGH)


def norm_parts(values):
    center = values - jnp.mean(values, axis=-1, keepdims=True)
    inv_std = lax.rsqrt(jnp.mean(center * center, axis=-1, keepdims=True) + 1e-05)
    return center * inv_std, inv_std


def folded(values):
    return jnp.sum(values.reshape(values.shape[0] // 8, 8, values.shape[1]), axis=0)


def flipped(value, step):
    return value + step * (1 - 2 * lax.rem(value // step, 2))


def peers():
    d, t = lax.axis_index("dp"), lax.axis_index("tensor")
    return {"core": (d, flipped(t, 1)), "y": (d, flipped(t, 2)), "far": (d, 3 - t)}


def greet(devices):
    barrier = pltpu.get_barrier_semaphore()
    for device in devices:
        pl.semaphore_signal(barrier, inc=1, device_id=device, device_id_type=MESH)
    pl.semaphore_wait(barrier, len(devices))


class Copies:
    def __init__(self, send, recv, local):
        self.send, self.recv, self.local = send, recv, local
        self.remotes, self.locals = [], 0

    def to(self, source, target, device):
        slot = len(self.remotes)
        assert slot < self.send.shape[0]
        made = pltpu.make_async_remote_copy(
            src_ref=source,
            dst_ref=target,
            send_sem=self.send.at[slot],
            recv_sem=self.recv.at[slot],
            device_id=device,
            device_id_type=MESH,
        )
        made.start()
        self.remotes.append(made)
        return made

    def move(self, source, target):
        assert self.locals < self.local.shape[0]
        made = pltpu.make_async_copy(source, target, self.local.at[self.locals])
        made.start()
        self.locals += 1
        return made

    def drain(self):
        for made in self.remotes:
            made.wait_send()


def softmax(scores, allowed):
    scores = jnp.where(allowed, scores * SCALING, -1000000000.0)
    exponent = jnp.exp(scores - jnp.max(scores, axis=-1, keepdims=True))
    return exponent / jnp.sum(exponent, axis=-1, keepdims=True)


def window_allowed(length, window):
    row = lax.broadcasted_iota(jnp.int32, (window, window), 0)
    column = lax.broadcasted_iota(jnp.int32, (window, window), 1)
    return (row // length == column // length) & (row >= column)


def head(j):
    return pl.ds(j * HEAD_SIZE, HEAD_SIZE)


def lanes(j):
    return slice(j * HEAD_SIZE, (j + 1) * HEAD_SIZE)


VEC = ("ln1g", "ln1b", "sob", "ln2g", "ln2b", "cob", "ln3g", "ln3b", "mob")


def forward_kernel(dims, *refs):
    captions, length, images, width, part = dims
    rows = captions * length
    (counts, vec, tokens, image, bias, *weights), refs = refs[:12], refs[12:]
    (q1, kv1, o1, x1, q2, kv2, o2, x2, img, w_back, kv_turned, w_in, w_out, bias_all), refs = (
        refs[:14],
        refs[14:],
    )
    (
        (v_q1, v_kv1, v_o1, v_x1, v_q2, v_kv2, v_o2, v_x2, v_img),
        v_w,
        v_turned,
        v_tokens,
        v_h,
        send,
        recv,
        local,
    ) = refs
    w_keep = list(v_w) + [w_in, w_out]
    d, t = lax.axis_index("dp"), lax.axis_index("tensor")
    near = {"p0": (flipped(d, 1), t), "p1": (flipped(d, 2), t), **peers()}
    order = [t, flipped(t, 1), flipped(t, 2), 3 - t]
    copies = Copies(send, recv, local)
    token_load = copies.move(tokens.at[pl.ds(t * rows, rows)], v_tokens)
    loads = [copies.move(weights[k], v_w[k].at[t]) for k in range(5)]
    image_load = copies.move(image.at[pl.ds(t * captions, captions)], v_img.at[:, t])
    greet(list(near.values()))
    quarter = lax.rem(d, 4)
    quarters = (quarter, flipped(quarter, 1), flipped(quarter, 2), 3 - quarter)
    other = order[2]

    def part_of(k, which, half=None):
        size = weights[k].shape[0] // 4
        start = quarters[which] * size
        if half is not None:
            first = (size // 2 + 15) // 16 * 16
            start, size = (start, first) if half == 0 else (start + first, size - first)
        return pl.ds(pl.multiple_of(start, 16), size)

    def region(k, which, half=None):
        return w_keep[k].at[other, part_of(k, which, half)]

    count = len(weights)
    over_y, over, own_core, images_in = {}, {}, {}, []

    def send_y(k):
        over_y[k] = copies.to(
            weights[k].at[part_of(k, 0)], w_keep[k].at[t, part_of(k, 0)], near["y"]
        )

    def send_image(name, target):
        images_in.append(
            copies.to(image.at[pl.ds(target * captions, captions)], v_img.at[:, t], near[name])
        )

    own_core[0] = copies.to(weights[0], w_keep[0].at[t], near["core"])
    own_core[1] = copies.to(weights[1], w_keep[1].at[t], near["core"])
    for k in range(6):
        send_y(k)
    send_image("y", order[2])
    send_image("far", order[3])
    send_y(6)
    send_image("core", order[1])
    for k in range(2, count):
        own_core[k] = copies.to(weights[k], w_keep[k].at[t], near["core"])
    biases = [copies.to(bias, bias_all.at[t], near[name]) for name in ("core", "y", "far")]
    core = {k: [] for k in range(count)}

    def first(k):
        over_y[k].wait_recv()
        over[k, 0] = copies.to(region(k, 0), region(k, 0), near["p0"])
        over[k, 1] = copies.to(region(k, 0), region(k, 0), near["p1"])
        core[k].append(copies.to(region(k, 0), region(k, 0), near["core"]))

    def second(k):
        over[k, 0].wait_recv()
        over[k, 2] = copies.to(region(k, 1, 0), region(k, 1, 0), near["p1"])
        core[k].append(copies.to(region(k, 1), region(k, 1), near["core"]))
        over[k, 1].wait_recv()
        over[k, 3] = copies.to(region(k, 2, 1), region(k, 2, 1), near["p0"])
        core[k].append(copies.to(region(k, 2), region(k, 2), near["core"]))

    def third(k):
        over[k, 2].wait_recv()
        core[k].append(copies.to(region(k, 3, 0), region(k, 3, 0), near["core"]))
        over[k, 3].wait_recv()
        core[k].append(copies.to(region(k, 3, 1), region(k, 3, 1), near["core"]))

    def arrived(k):
        for made in core[k]:
            made.wait_recv()

    g = {name: vec[i : i + 1, :] for i, name in enumerate(VEC)}
    slab = 32

    def normed(source, gain, shift):
        def body(i, carry):
            place = pl.ds(pl.multiple_of(i * slab, slab), slab)
            n, _ = norm_parts(source[place, :].astype(HIGH))
            v_h[place, :] = (n * gain + shift).astype(LOW)
            return carry

        lax.fori_loop(0, rows // slab, body, 0)

    token_load.wait()
    normed(v_tokens, g["ln1g"], g["ln1b"])

    def start_sum(target, source, shift):
        def body(i, carry):
            place = pl.ds(pl.multiple_of(i * slab, slab), slab)
            target[place, :] = source[place, :].astype(HIGH) + shift
            return carry

        lax.fori_loop(0, rows // slab, body, 0)

    start_sum(v_x1, v_tokens, g["sob"])
    window = 2 * length
    causal = window_allowed(length, window)
    heads = part // HEAD_SIZE

    def self_part(s):
        h = v_h[...]
        v_q1[s] = dot_rows(h, v_w[0][s, :part, :]).astype(LOW)
        v_kv1[s] = dot_rows(v_w[0][s, part:, :], h).astype(LOW)
        for w in range(rows // window):
            span = pl.ds(w * window, window)
            mixed = []
            for j in range(heads):
                q = v_q1[s, span, :][:, lanes(j)]
                p = softmax(dot(q, v_kv1[s, head(j), span]), causal)
                mixed.append(dot_rows(p.astype(LOW), v_kv1[s, head(heads + j), span]))
            v_o1[s, span, :] = jnp.concatenate(mixed, axis=1).astype(LOW)
        v_x1[...] += dot(v_o1[s], v_w[1][s])

    def queries(s):
        v_q2[s] = dot_rows(v_h[...], v_w[2][s]).astype(LOW)

    def turn(s):
        v_turned[:, pl.ds(pl.multiple_of(s * 2 * part, 128), 2 * part)] = v_w[3][s].T

    def cross_part(s):
        def body(c, carry):
            span = pl.ds(pl.multiple_of(c * images, images), images)
            v_kv2[s, :, span] = dot(v_w[3][s], v_img[c].reshape(width, images)).astype(LOW)
            own = pl.ds(pl.multiple_of(c * length, length), length)
            allowed = (
                lax.broadcasted_iota(jnp.int32, (length, images), 1)
                < counts[t * captions + c]
            )
            mixed = []
            for j in range(heads):
                q = v_q2[s, own, :][:, lanes(j)]
                p = softmax(dot(q, v_kv2[s, head(j), span]), allowed)
                mixed.append(dot_rows(p.astype(LOW), v_kv2[s, head(heads + j), span]))
            v_o2[s, own, :] = jnp.concatenate(mixed, axis=1).astype(LOW)
            return carry

        lax.fori_loop(0, captions, body, 0)
        v_x2[...] += dot(v_o2[s], v_w[4][s])

    back = []
    loads[0].wait()
    loads[1].wait()
    self_part(order[0])
    own_core[0].wait_recv()
    own_core[1].wait_recv()
    first(0)
    self_part(order[1])
    first(1)
    first(2)
    second(0)
    first(3)
    second(1)
    first(4)
    third(0)
    second(2)
    third(1)
    second(3)
    arrived(0)
    arrived(1)
    self_part(order[2])
    third(2)
    second(4)
    self_part(order[3])
    first(5)
    third(3)
    third(4)
    back.append(copies.move(v_q1, q1))
    back.append(copies.move(v_kv1, kv1))
    back.append(copies.move(v_o1, o1))
    back.append(copies.move(v_x1, x1))
    normed(v_x1, g["ln2g"], g["ln2b"])
    start_sum(v_x2, v_x1, g["cob"])
    for k in range(2, 5):
        loads[k].wait()
        own_core[k].wait_recv()
        arrived(k)
    for s in order:
        queries(s)
        turn(s)
    back.append(copies.move(v_turned, kv_turned))
    for i, k in enumerate((0, 1, 2, 4)):
        back.append(copies.move(v_w[k], w_back[i]))
    second(5)
    third(5)
    image_load.wait()
    for made in images_in:
        made.wait_recv()
    back.append(copies.move(v_q2, q2))
    back.append(copies.move(v_img, img))
    cross_part(order[0])
    first(6)
    cross_part(order[1])
    cross_part(order[2])
    second(6)
    cross_part(order[3])
    back.append(copies.move(v_kv2, kv2))
    back.append(copies.move(v_o2, o2))
    back.append(copies.move(v_x2, x2))
    third(6)
    for k in (5, 6):
        own_core[k].wait_recv()
        arrived(k)
    for made in biases:
        made.wait_recv()
    copies.drain()
    for made in back:
        made.wait()


def forward(dims, counts, vec, tokens, image, bias, weights):
    captions, length, images, width, part = dims
    rows = captions * length
    shape = jax.ShapeDtypeStruct
    kept = [
        ((4, rows, part), LOW),
        ((4, 2 * part, rows), LOW),
        ((4, rows, part), LOW),
        ((rows, width), HIGH),
        ((4, rows, part), LOW),
        ((4, 2 * part, captions * images), LOW),
        ((4, rows, part), LOW),
        ((rows, width), HIGH),
        ((captions, 4, part, images), LOW),
    ]
    sizes = [(4, *w.shape) for w in weights]
    any_spec = pl.BlockSpec(memory_space=pl.ANY)
    vmem, smem = pl.BlockSpec(memory_space=pltpu.VMEM), pl.BlockSpec(memory_space=pltpu.SMEM)
    remote = 7 * 12 + 6
    return pl.pallas_call(
        partial(forward_kernel, dims),
        out_shape=[shape(*k) for k in kept]
        + [
            [shape(sizes[k], LOW) for k in (0, 1, 2, 4)],
            shape((width, 8 * part), LOW),
            shape(sizes[5], LOW),
            shape(sizes[6], LOW),
            shape((4, *bias.shape), HIGH),
        ],
        in_specs=[smem, vmem] + [any_spec] * 10,
        out_specs=[any_spec] * 9 + [[any_spec] * 4] + [any_spec] * 4,
        scratch_shapes=[
            [pltpu.VMEM(*k) for k in kept],
            [pltpu.VMEM(sizes[k], LOW) for k in range(5)],
            pltpu.VMEM((width, 8 * part), LOW),
            pltpu.VMEM((rows, width), LOW),
            pltpu.VMEM((rows, width), LOW),
            pltpu.SemaphoreType.DMA((remote,)),
            pltpu.SemaphoreType.DMA((remote,)),
            pltpu.SemaphoreType.DMA((32,)),
        ],
        name="forward",
        compiler_params=pltpu.CompilerParams(
            collective_id=0, has_side_effects=True, vmem_limit_bytes=62 << 20
        ),
    )(counts, vec, tokens, image, bias, *weights)


def backward_kernel(dims, stride, plan, *refs):
    captions, length, images, width, part = dims
    rows = captions * length
    block = width // 8
    heads = part // HEAD_SIZE
    window = 2 * length
    (
        (counts, vec, bias, bias_all, tokens, grads, raw_in, raw_out),
        (q1, kv1, o1, x1, q2, kv2, o2, x2, img),
        w_back,
        kv_turned,
        w_in,
        w_out,
        sums,
        image_out,
        out_all,
        token_all,
        small_out,
        (v_q1, v_kv1, v_o1, v_x1, v_q2, v_kv2, v_o2, v_x2, v_img),
        (v_w0, v_w1, v_w2, v_w4),
        v_turned,
        v_in,
        v_out,
        v_bias,
        v_tokens,
        v_grads,
        g_out,
        g_in,
        v_h,
        v_turn_a,
        v_turn_b,
        v_f0,
        v_f1,
        v_y,
        v_g,
        v_small_a,
        v_low,
        v_narrow,
        v_image,
        from_core,
        halves,
        from_y,
        result,
        v_sum,
        sum_in,
        credit,
        send,
        recv,
        local,
    ) = refs
    d, t = lax.axis_index("dp"), lax.axis_index("tensor")
    y, c = t // 2, lax.rem(t, 2)
    near = peers()
    bits = [lax.rem(d // (stride << b), 2) for b in range(3)]
    partner = [(flipped(d, stride << b), t) for b in range(3)]
    order = [3 - t, flipped(t, 2), flipped(t, 1), t]
    copies = Copies(send, recv, local)

    mine = pl.ds(t * rows, rows)
    load_x2 = copies.move(x2, v_x2)
    load_grads = copies.move(grads.at[mine], v_grads)
    load_mlp = []
    for i, s in enumerate(order):
        sources = (raw_in, raw_out, bias) if i == 3 else (
            w_in.at[s // 2, lax.rem(s, 2)],
            w_out.at[s // 2, lax.rem(s, 2)],
            bias_all.at[s],
        )
        targets = (v_in.at[s // 2, lax.rem(s, 2)], v_out.at[s // 2, lax.rem(s, 2)], v_bias.at[s])
        load_mlp.append([copies.move(a, b) for a, b in zip(sources, targets)])
    load_rest = [
        copies.move(a, b)
        for a, b in (
            (w_back[3], v_w4),
            (q2, v_q2),
            (kv2, v_kv2),
            (o2, v_o2),
            (x1, v_x1),
            (img, v_img),
            (w_back[2], v_w2),
            (kv_turned, v_turned),
            (w_back[1], v_w1),
            (w_back[0], v_w0),
            (q1, v_q1),
            (kv1, v_kv1),
            (o1, v_o1),
            (tokens.at[mine], v_tokens),
        )
    ]
    greet([*near.values(), *partner])

    g = {name: vec[i : i + 1, :] for i, name in enumerate(VEC)}
    slab = 32

    def loop(body, init, step=slab):
        def run(i, carry):
            return body(pl.ds(pl.multiple_of(i * step, step), step), carry)

        return lax.fori_loop(0, rows // step, run, init)

    zeros = jnp.zeros((8, width), HIGH)
    small_rows = {}

    def keep(name, total):
        v_sum[0, pl.ds(name, 1), :] = jnp.sum(total, axis=0, keepdims=True)

    units = [(p, o) for p in range(4) for o in (0, 1)]
    pieces = [g_out, g_in, v_in, v_out]
    to_core, hops, places = {}, {}, {}
    side = (1 - y, y)

    def offer(p, o):
        u = 2 * p + o
        if p >= 2:
            pl.semaphore_wait(credit.at[u - 4], 1)
        to_core[p, o] = copies.to(
            pieces[p].at[side[o], 1 - c], from_core.at[u % 4], near["core"]
        )

    def add(target, left, *others):
        lead = target.shape[:-2]
        total = 1
        for size in lead:
            total *= size
        tall = 32
        slabs = target.shape[-2] // tall

        def body(i, carry):
            index, rest = [], i // slabs
            for size in reversed(lead):
                index.insert(0, lax.rem(rest, size))
                rest = rest // size
            place = (*index, pl.ds(pl.multiple_of(lax.rem(i, slabs) * tall, tall), tall))
            value = left[place].astype(HIGH)
            for ref in others:
                value = value + ref[place].astype(HIGH)
            target[place] = value.astype(target.dtype)
            return carry

        lax.fori_loop(0, total * slabs, body, 0)

    def cut(bit, left, value):
        return tuple(value if b == bit else slice(None) for b in sorted(left, reverse=True))

    back = []

    def advance(p, o, stage):
        u = 2 * p + o
        turn = plan[p]
        y_first = turn[0] == "y"
        xyz = [b for b in turn if b != "y"]
        base = pieces[p].at[side[o], c]
        if stage == 0:
            to_core[p, o].wait_recv()
            if y_first and o == 1:
                hops[p, 0, "y"].wait_recv()
                add(base, base, from_core.at[u % 4], from_y[p])
            else:
                add(base, base, from_core.at[u % 4])
            if p < 2:
                pl.semaphore_signal(
                    credit.at[u], inc=1, device_id=near["core"], device_id_type=MESH
                )
            places[u] = base, [0, 1, 2]
            if y_first and o == 0:
                hops[p, 0, "y"] = copies.to(base, from_y[p], near["y"])
                return
        if stage > 0:
            source, left = places[u]
            bit = xyz[stage - 1]
            hops[p, o, stage].wait_recv()
            target = halves[stage - 1].at[u]
            kept = source.at[cut(bit, left, bits[bit])]
            remaining = [b for b in left if b != bit]
            last = stage == 3
            if last and o == 1:
                if y_first:
                    add(result.at[p], target, kept)
                else:
                    hops[p, 0, "y"].wait_recv()
                    add(result.at[p], target, kept, from_y[p])
                back.append(copies.move(result.at[p], sums[p]))
                return
            add(target, target, kept)
            places[u] = target, remaining
            if last:
                hops[p, 0, "y"] = copies.to(target, from_y[p], near["y"])
                return
        source, left = places[u]
        bit = xyz[stage]
        shape = halves[stage].at[u]
        hops[p, o, stage + 1] = copies.to(
            source.at[cut(bit, left, 1 - bits[bit])], shape, partner[bit]
        )

    def stages(p, o):
        return 1 if plan[p][0] == "y" and o == 0 else 4

    load_x2.wait()
    load_grads.wait()

    def start(place, carry):
        n, _ = norm_parts(v_x2[place, :])
        v_h[place, :] = (n * g["ln3g"] + g["ln3b"]).astype(LOW)
        v_y[place, :] = v_x2[place, :] + g["mob"]
        v_g[place, :] = jnp.zeros((slab, width), HIGH)
        return carry + folded(v_grads[place, :].astype(HIGH))

    keep(8, loop(start, zeros))
    v_turn_a[...] = v_h[...].T
    v_turn_b[...] = v_grads[...].T

    def weight(ref, s):
        return ref[s // 2, lax.rem(s, 2)].reshape(width, width)

    def put(ref, s, first, values):
        half, values = values
        ref[s // 2, lax.rem(s, 2), half, :, :, :, first : first + values.shape[1]] = (
            values.astype(LOW).reshape(2, 2, block, values.shape[1])
        )

    def half_rows(half):
        return pl.ds(half * (width // 2), width // 2)

    def feed(s):
        v_f0[...] = dot(v_h[...], weight(v_in, s))
        v_f1[...] = dot_rows(v_grads[...], weight(v_out, s))
        shift = v_bias[s]

        def act(place, carry):
            a = v_f0[place, :] + shift
            cumulative = 0.5 * (1.0 + lax.erf(a * (0.5**0.5)))
            density = jnp.exp(-0.5 * a * a) * 0.3989422804014327
            v_low[0, place, :] = (a * cumulative).astype(LOW)
            ga = (v_f1[place, :] * (cumulative + a * density)).astype(LOW)
            v_low[1, place, :] = ga
            return carry + folded(ga.astype(HIGH))

        total = loop(act, zeros, 16)
        v_small_a[s] = jnp.sum(total, axis=0, keepdims=True)
        u, ga = v_low[0], v_low[1]
        v_y[...] += dot(u, weight(v_out, s))
        v_g[...] += dot_rows(ga, weight(v_in, s))
        for half in range(2):
            put(g_out, s, 0, (half, dot(v_turn_b[half_rows(half), :], u)))
            put(g_in, s, 0, (half, dot(v_turn_a[half_rows(half), :], ga)))

    for i, s in enumerate(order):
        for load in load_mlp[i]:
            load.wait()
        feed(s)
        if i == 0:
            offer(0, 0)
            offer(1, 0)
        if i == 1:
            advance(0, 0, 0)
            advance(1, 0, 0)
        if i == 2:
            offer(0, 1)
            offer(1, 1)

    def shared(source, target):
        place = target.at[pl.ds(t * rows, rows)]
        back.append(copies.move(source, place))
        return [copies.to(source, place, near[name]) for name in ("core", "y", "far")]

    def norm_back(source, gain, old, new, low):
        def body(place, carry):
            a, b, e = carry
            n, inv_std = norm_parts(source[place, :].astype(HIGH))
            gh = v_g[place, :]
            scaled = gh * gain
            grad = inv_std * (
                scaled
                - jnp.mean(scaled, axis=-1, keepdims=True)
                - n * jnp.mean(scaled * n, axis=-1, keepdims=True)
            )
            grad = old[place, :].astype(HIGH) + grad
            if new is not None:
                new[place, :] = grad
                e = e + folded(grad)
            low[place, :] = grad.astype(LOW)
            return a + folded(gh * n), b + folded(gh), e

        return loop(body, (zeros, zeros, zeros))

    def finish(place, carry):
        v_h[place, :] = v_y[place, :].astype(LOW)
        return carry

    advance(0, 0, 1)
    advance(1, 0, 1)
    advance(0, 1, 0)
    advance(1, 1, 0)
    loop(finish, 0)
    v_out_low = v_low.at[0]
    v_out_low[...] = v_h[...]
    out_moves = shared(v_out_low, out_all)
    gain_sum, bias_sum, total = norm_back(v_x2, g["ln3g"], v_grads, v_f0, v_grads)
    keep(6, gain_sum)
    keep(7, bias_sum)
    keep(5, total)

    for load in load_rest:
        load.wait()

    def again(source, gain, shift):
        def body(place, carry):
            n, _ = norm_parts(source[place, :].astype(HIGH))
            v_h[place, :] = (n * gain + shift).astype(LOW)
            v_g[place, :] = jnp.zeros((slab, width), HIGH)
            return carry

        loop(body, 0)

    again(v_x1, g["ln2g"], g["ln2b"])
    v_turn_a[...] = v_h[...].T
    v_turn_b[...] = v_grads[...].T
    go, gq = v_narrow.at[0], v_narrow.at[1]

    def attend_back(p, q, k, v, g_mix):
        low_p = p.astype(LOW)
        gp = dot(g_mix, v)
        inner = jnp.sum(gp * p, axis=-1, keepdims=True)
        gs = (p * (gp - inner)).astype(LOW)
        return (
            dot_rows(gs, k) * SCALING,
            (dot_columns(q, gs) * SCALING).astype(LOW),
            dot_columns(g_mix, low_p).astype(LOW),
        )

    def gradients(piece, s, of_keys, o_kept):
        for half in range(2):
            put(piece, s, 0, (half, of_keys(half)))
            both = [dot(v_turn_a[half_rows(half), :], gq[...])]
            both.append(dot(v_turn_b[half_rows(half), :], o_kept[s]))
            put(piece, s, 2 * part, (half, jnp.concatenate(both, axis=1)))

    def cross_back(s):
        go[...] = dot_rows(v_grads[...], v_w4[s]).astype(LOW)

        def body(caption, carry):
            span = pl.ds(pl.multiple_of(caption * images, images), images)
            own = pl.ds(pl.multiple_of(caption * length, length), length)
            allowed = (
                lax.broadcasted_iota(jnp.int32, (length, images), 1)
                < counts[t * captions + caption]
            )
            all_q, all_go, queries = v_q2[s, own, :], go[own, :], []
            for j in range(heads):
                q, k, v = all_q[:, lanes(j)], v_kv2[s, head(j), span], v_kv2[s, head(heads + j), span]
                p = softmax(dot(q, k), allowed)
                g_q, g_k, g_v = attend_back(p, q, k, v, all_go[:, lanes(j)])
                queries.append(g_q)
                v_kv2[s, head(j), span] = g_k
                v_kv2[s, head(heads + j), span] = g_v
            gq[own, :] = jnp.concatenate(queries, axis=1).astype(LOW)
            return carry

        lax.fori_loop(0, captions, body, 0)
        v_g[...] += dot(gq[...], v_w2[s])

        def of_keys(half):
            total = 0
            for caption in range(captions):
                span = slice(caption * images, (caption + 1) * images)
                features = v_img[caption, 2 * half : 2 * half + 2].reshape(width // 2, images)
                total = total + dot_rows(features, v_kv2[s, :, span])
            return total

        gradients(v_in, s, of_keys, v_o2)

    for i, s in enumerate(order):
        cross_back(s)
        if i == 0:
            offer(2, 0)
            advance(0, 1, 1)
            advance(1, 1, 1)
            advance(0, 0, 2)
        if i == 1:
            advance(1, 0, 2)
            advance(2, 0, 0)
            advance(0, 0, 3)
        if i == 2:
            offer(2, 1)
            advance(1, 0, 3)
            advance(0, 1, 2)
        if i == 3:
            advance(1, 1, 2)
            if stages(2, 0) > 1:
                advance(2, 0, 1)
    image_span = pl.ds(t * captions, captions)

    def image_part(caption, carry):
        span = pl.ds(pl.multiple_of(caption * images, images), images)
        values = dot(v_turned[...], v_kv2[:, :, span].reshape(8 * part, images))
        v_image[caption] = values.astype(LOW).reshape(4, part, images)
        return carry

    lax.fori_loop(0, captions, image_part, 0)
    advance(2, 1, 0)
    image_moves = [
        copies.to(v_image.at[:, target], image_out.at[image_span], near[name])
        for name, target in (("y", flipped(t, 2)), ("far", 3 - t), ("core", flipped(t, 1)))
    ]
    back.append(copies.move(v_image.at[:, t], image_out.at[image_span]))
    gain_sum, bias_sum, total = norm_back(v_x1, g["ln2g"], v_f0, v_f1, v_grads)
    keep(3, gain_sum)
    keep(4, bias_sum)
    keep(2, total)
    advance(0, 1, 3)
    advance(1, 1, 3)

    again(v_tokens, g["ln1g"], g["ln1b"])
    v_turn_a[...] = v_h[...].T
    v_turn_b[...] = v_grads[...].T
    causal = window_allowed(length, window)

    def self_back(s):
        go[...] = dot_rows(v_grads[...], v_w1[s]).astype(LOW)
        for w in range(rows // window):
            span = pl.ds(w * window, window)
            all_q, all_go, queries = v_q1[s, span, :], go[span, :], []
            for j in range(heads):
                q, k, v = all_q[:, lanes(j)], v_kv1[s, head(j), span], v_kv1[s, head(heads + j), span]
                p = softmax(dot(q, k), causal)
                g_q, g_k, g_v = attend_back(p, q, k, v, all_go[:, lanes(j)])
                queries.append(g_q)
                v_kv1[s, head(j), span] = g_k
                v_kv1[s, head(heads + j), span] = g_v
            gq[span, :] = jnp.concatenate(queries, axis=1).astype(LOW)
        v_g[...] += dot(gq[...], v_w0[s, :part, :]) + dot_columns(v_kv1[s], v_w0[s, part:, :])

        def of_keys(half):
            return dot_rows(v_turn_a[half_rows(half), :], v_kv1[s])

        gradients(v_out, s, of_keys, v_o1)

    for i, s in enumerate(order):
        self_back(s)
        if i == 0:
            offer(3, 0)
            if stages(2, 0) > 1:
                advance(2, 0, 2)
            advance(2, 1, 1)
        if i == 1:
            advance(3, 0, 0)
        if i == 2:
            offer(3, 1)
            if stages(2, 0) > 1:
                advance(2, 0, 3)
            advance(2, 1, 2)
        if i == 3:
            if stages(3, 0) > 1:
                advance(3, 0, 1)
    advance(3, 1, 0)
    gain_sum, bias_sum, _ = norm_back(v_tokens, g["ln1g"], v_f1, None, v_h)
    keep(0, gain_sum)
    keep(1, bias_sum)
    token_moves = shared(v_h, token_all)
    for s in range(4):
        v_sum[0, 9 + s : 10 + s, :] = v_small_a[s]
    v_sum[0, 13:16, :] = jnp.zeros((3, width), HIGH)
    small_to = [near["core"], *partner, near["y"]]

    def total_step(i):
        made = copies.to(v_sum.at[i], sum_in.at[i], small_to[i])
        made.wait_recv()
        v_sum[i + 1] = v_sum[i] + sum_in[i]

    advance(2, 1, 3)
    total_step(0)
    total_step(1)
    if stages(3, 0) > 1:
        advance(3, 0, 2)
    advance(3, 1, 1)
    total_step(2)
    total_step(3)
    if stages(3, 0) > 1:
        advance(3, 0, 3)
    advance(3, 1, 2)
    total_step(4)
    back.append(copies.move(v_sum.at[5], small_out))
    advance(3, 1, 3)
    for made in out_moves + image_moves + token_moves:
        made.wait_recv()
    copies.drain()
    for made in back:
        made.wait()


def backward(dims, stride, counts, vec, bias, bias_all, tokens, grads, raw, kept, w_back, turned, mlp):
    captions, length, images, width, part = dims
    rows = captions * length
    block = width // 8
    plan = ((0, 1, 2, "y"), (1, 0, 2, "y"), ("y", 0, 1, 2), (0, 1, 2, "y"))
    shape = jax.ShapeDtypeStruct
    any_spec = pl.BlockSpec(memory_space=pl.ANY)
    vmem, smem = pl.BlockSpec(memory_space=pltpu.VMEM), pl.BlockSpec(memory_space=pltpu.SMEM)
    whole = (2, 2, 2, 2, 2, block, width)
    raw = [w.reshape(whole[2:]) for w in raw]
    mlp = [w.reshape(whole) for w in mlp]
    remote = 8 * 6 + 4 * 3 + 5

    def scratch(*size, dtype=LOW):
        return pltpu.VMEM(size, dtype)

    flat = [scratch(*k.shape, dtype=k.dtype) for k in kept]
    return pl.pallas_call(
        lambda *refs: backward_kernel(
            dims,
            stride,
            plan,
            refs[:8],
            refs[8:17],
            refs[17:21],
            refs[21],
            refs[22],
            refs[23],
            refs[24:28],
            *refs[28:],
        ),
        out_shape=[shape((block, width), HIGH)] * 4
        + [
            shape((4 * captions, part, images), LOW),
            shape((4 * rows, width), LOW),
            shape((4 * rows, width), LOW),
            shape((16, width), HIGH),
        ],
        in_specs=[smem, vmem] + [any_spec] * 22,
        out_specs=[any_spec] * 8,
        scratch_shapes=[
            flat,
            [scratch(*w.shape) for w in w_back],
            scratch(*turned.shape),
            scratch(*whole),
            scratch(*whole),
            scratch(4, 1, width, dtype=HIGH),
            scratch(rows, width),
            scratch(rows, width),
            scratch(*whole),
            scratch(*whole),
            scratch(rows, width),
            scratch(width, rows),
            scratch(width, rows),
            scratch(rows, width, dtype=HIGH),
            scratch(rows, width, dtype=HIGH),
            scratch(rows, width, dtype=HIGH),
            scratch(rows, width, dtype=HIGH),
            scratch(4, 1, width, dtype=HIGH),
            scratch(2, rows, width),
            scratch(2, rows, part),
            scratch(captions, 4, part, images),
            scratch(4, 2, 2, 2, block, width),
            [
                scratch(8, 2, 2, block, width),
                scratch(8, 2, block, width),
                scratch(8, block, width),
            ],
            [
                scratch(*((2, 2, 2) if turn[0] == "y" else ()), block, width)
                for turn in plan
            ],
            scratch(4, block, width, dtype=HIGH),
            scratch(6, 16, width, dtype=HIGH),
            scratch(5, 16, width, dtype=HIGH),
            pltpu.SemaphoreType.REGULAR((4,)),
            pltpu.SemaphoreType.DMA((remote,)),
            pltpu.SemaphoreType.DMA((remote,)),
            pltpu.SemaphoreType.DMA((48,)),
        ],
        name="backward",
        compiler_params=pltpu.CompilerParams(
            collective_id=1, has_side_effects=True, vmem_limit_bytes=67043328
        ),
    )(counts, vec, bias, bias_all, tokens, grads, *raw, *kept, *w_back, turned, *mlp)


def local(
    tokens,
    image_tokens,
    image_counts,
    ln1_gain,
    ln1_bias,
    self_qkv,
    self_output_weight,
    self_output_bias,
    ln2_gain,
    ln2_bias,
    cross_query_weight,
    cross_kv,
    cross_output_weight,
    cross_output_bias,
    ln3_gain,
    ln3_bias,
    mlp_in,
    mlp_in_bias,
    mlp_out,
    mlp_out_bias,
    grad_out,
):
    stride = lax.axis_size("dp") // 8
    all_captions, length, width = tokens.shape
    images, part = image_tokens.shape[1:]
    captions = all_captions // 4
    dims = (captions, length, images, width, part)
    rows = [
        ln1_gain,
        ln1_bias,
        self_output_bias,
        ln2_gain,
        ln2_bias,
        cross_output_bias,
        ln3_gain,
        ln3_bias,
        mlp_out_bias,
    ]
    vec = jnp.concatenate([jnp.stack(rows), jnp.zeros((7, width), HIGH)])
    tokens = tokens.reshape(-1, width)
    grads = grad_out.reshape(-1, width)
    bias = mlp_in_bias.reshape(1, -1)
    weights = [
        self_qkv.transpose(1, 2, 0).reshape(3 * part, width),
        self_output_weight,
        cross_query_weight.T,
        cross_kv.transpose(1, 2, 0).reshape(2 * part, width),
        cross_output_weight,
        mlp_in,
        mlp_out,
    ]
    *kept, w_back, turned, w_in, w_out, bias_all = forward(
        dims, image_counts, vec, tokens, image_tokens.transpose(0, 2, 1), bias, weights
    )
    sum_out, sum_in, sum_cross, sum_self, grad_image, output, grad_tokens, small = backward(
        dims,
        stride,
        image_counts,
        vec,
        bias,
        bias_all,
        tokens,
        grads,
        (mlp_in, mlp_out),
        kept,
        w_back,
        turned,
        (w_in, w_out),
    )
    if stride > 1:
        groups = [[hi * stride + lo for lo in range(stride)] for hi in range(8)]
        sum_out, sum_in, sum_cross, sum_self = (
            lax.psum_scatter(s, "dp", scatter_dimension=0, axis_index_groups=groups, tiled=True)
            for s in (sum_out, sum_in, sum_cross, sum_self)
        )
        small = lax.psum(small, "dp", axis_index_groups=groups)
    own_bias = lax.dynamic_index_in_dim(small, 9 + lax.axis_index("tensor"), 0, keepdims=False)
    keys, rest = slice(0, part), slice(part, 2 * part)
    third, fourth = slice(2 * part, 3 * part), slice(3 * part, 4 * part)
    return (
        output.reshape(all_captions, length, width),
        grad_tokens.reshape(all_captions, length, width),
        grad_image.transpose(0, 2, 1),
        small[0],
        small[1],
        jnp.stack([sum_self[:, third], sum_self[:, keys], sum_self[:, rest]], axis=1),
        sum_self[:, fourth].T,
        small[2],
        small[3],
        small[4],
        sum_cross[:, third],
        sum_cross[:, : 2 * part].reshape(-1, 2, part),
        sum_cross[:, fourth].T,
        small[5],
        small[6],
        small[7],
        sum_in,
        own_bias,
        sum_out.T,
        small[8],
    )


def solution(mesh):
    return jax.shard_map(
        local,
        mesh=mesh,
        in_specs=(
            P("dp", None, None),
            P("dp", None, "tensor"),
            P("dp"),
            P(),
            P(),
            P(None, None, "tensor"),
            P("tensor", None),
            P(),
            P(),
            P(),
            P(None, "tensor"),
            P(None, None, "tensor"),
            P("tensor", None),
            P(),
            P(),
            P(),
            P(None, "tensor"),
            P("tensor"),
            P("tensor", None),
            P(),
            P("dp", None, None),
        ),
        out_specs=(
            P("dp", None, None),
            P("dp", None, None),
            P("dp", None, "tensor"),
            P(),
            P(),
            P("dp", None, "tensor"),
            P("tensor", "dp"),
            P(),
            P(),
            P(),
            P("dp", "tensor"),
            P("dp", None, "tensor"),
            P("tensor", "dp"),
            P(),
            P(),
            P(),
            P("dp", "tensor"),
            P("tensor"),
            P("tensor", "dp"),
            P(),
        ),
        check_vma=False,
    )
```

time: 964 us -> 248 us (0.26)
  waiting for transfers between devices: 659 us -> 0 us
  Pallas kernels: 0 us -> 226 us
  matrix products: 105 us -> 0 us
  other arithmetic: 54.1 us -> 0.73 us
  local copies, waits for them, and re-layouts: 71.6 us -> 20.3 us
  blocking collectives: 38.2 us -> 0 us
  between operations: 15 us -> 0.72 us
  starting transfers between devices: 13.1 us -> 0 us
    reduce_scatter x5 -> x0, waiting for transfers between devices: 298 us -> none  [the longest x1 73 us: local(): lax.psum_scatter(grad_mlp_out_local, 'dp', scatter_dimension=1, tiled=True)]
    pallas_call x0 -> x2, Pallas kernels: none -> 226 us  [the longest x1 152 us: backward(): pl.pallas_call(lambda *refs: backward_kernel(dims, stride, plan, refs[:8]...]
    psum x5 -> x0, waiting for transfers between devices: 214 us -> none  [the longest x3 153 us: branch_total(): lax.psum(term_rows.astype(jnp.bfloat16), 'tensor').astype(jnp.float32)]
    unnamed x17 -> x0, waiting for transfers between devices: 107 us -> none
    dot_general x30 -> x0, matrix products: 101 us -> none  [the longest x1 10.3 us: local(): jnp.einsum('rd,fd->rf', grad_low, mlp_out, preferred_element_type=jnp.flo...]
    all_gather x1 -> x0, waiting for transfers between devices: 39 us -> none  [local(): image_full = lax.all_gather(image_tokens, 'tensor', axis=2, tiled=True)]
    psum x1 -> x0, blocking collectives: 38.2 us -> none  [local(): lax.psum((grad_gain_one, grad_bias_one, grad_self_bias, grad_gain_two, gr...]
    reduce_sum x12 -> x0, other arithmetic: 29.9 us -> none  [the longest x3 6.7 us: norm_parts(): center = values - jnp.mean(values, axis=-1, keepdims=True)]
  transfers between devices with their start and end apart: 14 -> 0, of which waited for: 13 -> 0; matrix products, arithmetic and copies ran while one was open for 13% -> 0% of each run, Pallas kernels for 0% -> 0%
where the time goes in v1:
time: 248 us
  Pallas kernels  226 us (91%)
  local copies, waits for them, and re-layouts  20.3 us (8%)
    pallas_call x1, Pallas kernels, backward(): pl.pallas_call(lambda *refs: backward_kernel(dims, stride, plan, refs[:8]...  152 us
    pallas_call x1, Pallas kernels, forward(): pl.pallas_call(partial(forward_kernel, dims), out_shape=[shape(*k) for k...  73.9 us
    unnamed x21, local copies, waits for them, and re-layouts  8.02 us
    another operation x9, local copies, waits for them, and re-layouts, local(): vec = jnp.concatenate([jnp.stack(rows), jnp.zeros((7, width), HIGH)])  6.2 us

profile of v1, /device:TPU:0, one launch (start us, length us, event | category | flops | bytes accessed | tf_op | source)
XLA Modules:
  0.0 247.7 jit_solution(16141399769405738381)
XLA Ops:
  0.7 0.7 stack.39
  1.3 0.7 stack.40
  2.0 0.7 stack.41
  2.7 0.7 stack.42
  3.4 0.7 stack.43
  4.1 0.7 stack.44
  4.8 0.7 stack.45
  5.5 0.7 stack.46
  6.2 0.7 stack.47
  6.9 1.3 concatenate.3.refs_1_
  8.1 1.3 reshape.76.refs_4_.refs_2_
  9.4 73.9 %forward.1 = (bf16[4,256,192]{2,1,0:T(8,128)(2,1)}, bf16[4,384,256]{2,1,0:T(8,128)(2,1)}, bf16[4,256,192]{2,1,0:T(8,128)(2,1)}, f32[256,768]{1,0:T(8,128)}, bf16...) custom-call(s32[16]{0:T(128)} %refs_0_.3, ...), custom_call_target="tpu_custom_call" | custom-call | tf_op jit(solution)/shard_map/forward/pallas_call | solution.py:359
  83.4 152.0 %backward.1 = (f32[96,768]{1,0:T(8,128)}, f32[96,768]{1,0:T(8,128)}, f32[96,768]{1,0:T(8,128)}, f32[96,768]{1,0:T(8,128)}, bf16[16,192,256]{2,1,0:T(8,128)(2,1)}...) custom-call(s32[16]{0:T(128)} %refs_0_.3, f32[16,768]{1,0:T(8,128)} %concatenate.3.refs_1_, ...), custom_call_target="tpu_custom_call" | custom-call | tf_op jit(solution)/shard_map/backward/pallas_call | solution.py:896
  235.3 0.0 copy-start.3
  235.3 0.0 copy-start.6
  235.3 0.0 copy-start.2
  235.4 2.0 slice_bitcast_fusion
  237.4 0.7 pad_maximum_fusion
  238.1 0.7 copy.41
  238.8 0.7 copy.42
  239.6 0.0 copy-done.3
  239.6 0.9 reshape.87
  240.5 0.0 copy-done.6
  240.5 0.7 slice_reduce_fusion
  241.1 0.0 copy-done.2
  241.1 1.1 copy.48
  242.3 0.8 copy-done.1
  243.1 1.1 copy.49
  244.3 0.8 copy-done
  245.1 1.1 copy.50
  246.2 0.7 copy.51
  247.0 0.7 copy.52
  (8 shorter events, 0.0 us)
Async XLA Ops:
  235.3 4.3 %copy-start.3 = (f32[96,768]{1,0:T(8,128)S(1)}, f32[96,768]{1,0:T(8,128)}, u32[]{:S(2)}) copy-start(f32[96,768]{1,0:T(8,128)} %get-tuple-element.67) | copy-start | bytes 884740
  235.3 5.1 %copy-start.6 = (f32[16,768]{1,0:T(8,128)S(1)}, f32[16,768]{1,0:T(8,128)}, u32[]{:S(2)}) copy-start(f32[16,768]{1,0:T(8,128)} %get-tuple-element.65) | copy-start | bytes 147460
  235.3 5.8 %copy-start.2 = (bf16[1024,768]{1,0:T(8,128)(2,1)S(1)}, bf16[1024,768]{1,0:T(8,128)(2,1)}, u32[]{:S(2)}) copy-start(bf16[1024,768]{1,0:T(8,128)(2,1)} %get-tuple-element.62) | copy-start | bytes 4718596
  241.1 2.0 copy-start.1
  243.1 2.0 copy-start
  245.1 1.1 copy-start.5
  245.1 1.9 copy-start.4

commit v2 on v1

v2 whole, which is shorter than its diff:
```python
from functools import partial

import jax
import jax.numpy as jnp
from jax import lax
from jax.experimental import pallas as pl
from jax.experimental.pallas import tpu as pltpu
from jax.sharding import PartitionSpec as P

HEAD_SIZE = 64
LOW = jnp.bfloat16
HIGH = jnp.float32
MESH = pl.DeviceIdType.MESH
SCALING = HEAD_SIZE**-0.5


def dot(left, right):
    return jnp.dot(left, right, preferred_element_type=HIGH)


def dot_rows(left, right):
    return lax.dot_general(left, right, (((1,), (1,)), ((), ())), preferred_element_type=HIGH)


def dot_columns(left, right):
    return lax.dot_general(left, right, (((0,), (0,)), ((), ())), preferred_element_type=HIGH)


def norm_parts(values):
    center = values - jnp.mean(values, axis=-1, keepdims=True)
    inv_std = lax.rsqrt(jnp.mean(center * center, axis=-1, keepdims=True) + 1e-05)
    return center * inv_std, inv_std


def folded(values):
    return jnp.sum(values.reshape(values.shape[0] // 8, 8, values.shape[1]), axis=0)


def flipped(value, step):
    return value + step * (1 - 2 * lax.rem(value // step, 2))


def peers():
    d, t = lax.axis_index("dp"), lax.axis_index("tensor")
    return {"core": (d, flipped(t, 1)), "y": (d, flipped(t, 2)), "far": (d, 3 - t)}


def greet(devices):
    barrier = pltpu.get_barrier_semaphore()
    for device in devices:
        pl.semaphore_signal(barrier, inc=1, device_id=device, device_id_type=MESH)
    pl.semaphore_wait(barrier, len(devices))


class Copies:
    def __init__(self, send, recv, local):
        self.send, self.recv, self.local = send, recv, local
        self.remotes, self.locals = [], 0

    def to(self, source, target, device):
        slot = len(self.remotes)
        assert slot < self.send.shape[0]
        made = pltpu.make_async_remote_copy(
            src_ref=source,
            dst_ref=target,
            send_sem=self.send.at[slot],
            recv_sem=self.recv.at[slot],
            device_id=device,
            device_id_type=MESH,
        )
        made.start()
        self.remotes.append(made)
        return made

    def move(self, source, target):
        assert self.locals < self.local.shape[0]
        made = pltpu.make_async_copy(source, target, self.local.at[self.locals])
        made.start()
        self.locals += 1
        return made

    def drain(self):
        for made in self.remotes:
            made.wait_send()


def softmax(scores, allowed):
    scores = jnp.where(allowed, scores * SCALING, -1000000000.0)
    exponent = jnp.exp(scores - jnp.max(scores, axis=-1, keepdims=True))
    return exponent / jnp.sum(exponent, axis=-1, keepdims=True)


def window_allowed(length, window, heads):
    row = lax.rem(lax.broadcasted_iota(jnp.int32, (heads * window, window), 0), window)
    column = lax.broadcasted_iota(jnp.int32, (heads * window, window), 1)
    return (row // length == column // length) & (row >= column)


def head_masks(width, dtype):
    lane = lax.broadcasted_iota(jnp.int32, (1, width), 1) // HEAD_SIZE
    return [(lane == j).astype(dtype) for j in range(width // HEAD_SIZE)]


def spread(values, masks):
    return jnp.concatenate([values * mask for mask in masks], axis=0)


def gathered(values, masks):
    n = values.shape[0] // len(masks)
    total = 0
    for j, mask in enumerate(masks):
        total = total + values[j * n : (j + 1) * n] * mask
    return total


FORWARD_VEC = ("ln1g", "ln1b", "sob", "ln2g", "ln2b", "cob")
BACKWARD_VEC = ("ln1g", "ln1b", "ln2g", "ln2b", "ln3g", "ln3b", "mob")


def as_rows(names, refs):
    return {name: ref[...].reshape(1, -1) for name, ref in zip(names, refs)}


def forward_kernel(dims, *refs):
    captions, length, images, width, part = dims
    rows = captions * length
    (counts, *vec), refs = refs[:7], refs[7:]
    (tokens, image, *weights), refs = refs[:7], refs[7:]
    (q1, kv1, o1, x1, q2, kv2, o2, x2, img, w_back, kv_turned), refs = refs[:11], refs[11:]
    (
        (v_q1, v_kv1, v_o1, v_x1, v_q2, v_kv2, v_o2, v_x2, v_img),
        v_w,
        v_turned,
        v_tokens,
        v_h,
        send,
        recv,
        local,
    ) = refs
    d, t = lax.axis_index("dp"), lax.axis_index("tensor")
    near = {"p0": (flipped(d, 1), t), "p1": (flipped(d, 2), t), **peers()}
    order = [t, flipped(t, 1), flipped(t, 2), 3 - t]
    copies = Copies(send, recv, local)
    token_load = copies.move(tokens.at[pl.ds(t * rows, rows)], v_tokens)
    loads = [copies.move(weights[k], v_w[k].at[t]) for k in range(5)]
    image_load = copies.move(image.at[pl.ds(t * captions, captions)], v_img.at[:, t])
    g = as_rows(FORWARD_VEC, vec)
    greet(list(near.values()))
    quarter = lax.rem(d, 4)
    quarters = (quarter, flipped(quarter, 1), flipped(quarter, 2), 3 - quarter)
    other = order[2]

    def part_of(k, which, half=None):
        size = weights[k].shape[0] // 4
        start = quarters[which] * size
        if half is not None:
            first = (size // 2 + 15) // 16 * 16
            start, size = (start, first) if half == 0 else (start + first, size - first)
        return pl.ds(pl.multiple_of(start, 16), size)

    def region(k, which, half=None):
        return v_w[k].at[other, part_of(k, which, half)]

    count = len(weights)
    over_y, over, own_core = {}, {}, {}

    def send_y(k):
        over_y[k] = copies.to(
            weights[k].at[part_of(k, 0)], v_w[k].at[t, part_of(k, 0)], near["y"]
        )

    for k in range(count):
        own_core[k] = copies.to(weights[k], v_w[k].at[t], near["core"])
        send_y(k)
    images_in = [
        [
            copies.to(image.at[target * captions + caption], v_img.at[caption, t], near[name])
            for name, target in (("y", order[2]), ("far", order[3]), ("core", order[1]))
        ]
        for caption in range(captions)
    ]
    core = {k: [] for k in range(count)}

    def first(k):
        over_y[k].wait_recv()
        over[k, 0] = copies.to(region(k, 0), region(k, 0), near["p0"])
        over[k, 1] = copies.to(region(k, 0), region(k, 0), near["p1"])
        core[k].append(copies.to(region(k, 0), region(k, 0), near["core"]))

    def second(k):
        over[k, 0].wait_recv()
        over[k, 2] = copies.to(region(k, 1, 0), region(k, 1, 0), near["p1"])
        core[k].append(copies.to(region(k, 1), region(k, 1), near["core"]))
        over[k, 1].wait_recv()
        over[k, 3] = copies.to(region(k, 2, 1), region(k, 2, 1), near["p0"])
        core[k].append(copies.to(region(k, 2), region(k, 2), near["core"]))

    def third(k):
        over[k, 2].wait_recv()
        core[k].append(copies.to(region(k, 3, 0), region(k, 3, 0), near["core"]))
        over[k, 3].wait_recv()
        core[k].append(copies.to(region(k, 3, 1), region(k, 3, 1), near["core"]))

    def arrived(k):
        for made in core[k]:
            made.wait_recv()

    slab = 32

    def normed(source, gain, shift):
        def body(i, carry):
            place = pl.ds(pl.multiple_of(i * slab, slab), slab)
            n, _ = norm_parts(source[place, :].astype(HIGH))
            v_h[place, :] = (n * gain + shift).astype(LOW)
            return carry

        lax.fori_loop(0, rows // slab, body, 0)

    token_load.wait()
    normed(v_tokens, g["ln1g"], g["ln1b"])

    def start_sum(target, source, shift):
        def body(i, carry):
            place = pl.ds(pl.multiple_of(i * slab, slab), slab)
            target[place, :] = source[place, :].astype(HIGH) + shift
            return carry

        lax.fori_loop(0, rows // slab, body, 0)

    start_sum(v_x1, v_tokens, g["sob"])
    window = 2 * length
    heads = part // HEAD_SIZE
    causal = window_allowed(length, window, heads)
    masks, wide_masks = head_masks(part, LOW), head_masks(part, HIGH)

    def self_part(s):
        h = v_h[...]
        v_q1[s] = dot_rows(h, v_w[0][s, :part, :]).astype(LOW)
        v_kv1[s] = dot_rows(v_w[0][s, part:, :], h).astype(LOW)
        for w in range(rows // window):
            span = pl.ds(w * window, window)
            q = spread(v_q1[s, span, :], masks)
            p = softmax(dot(q, v_kv1[s, :part, span]), causal)
            mixed = dot_rows(p.astype(LOW), v_kv1[s, part:, span])
            v_o1[s, span, :] = gathered(mixed, wide_masks).astype(LOW)
        v_x1[...] += dot(v_o1[s], v_w[1][s])

    def queries(s):
        v_q2[s] = dot_rows(v_h[...], v_w[2][s]).astype(LOW)

    def turn(s):
        v_turned[:, pl.ds(pl.multiple_of(s * 2 * part, 128), 2 * part)] = v_w[3][s].T

    def cross_part(c):
        allowed = lax.broadcasted_iota(jnp.int32, (1, images), 1) < counts[t * captions + c]
        span, own = pl.ds(c * images, images), pl.ds(c * length, length)

        def body(s, carry):
            kv = dot(v_w[3][s], v_img[c].reshape(width, images)).astype(LOW)
            v_kv2[s, :, span] = kv
            q = spread(v_q2[s, own, :], masks)
            p = softmax(dot(q, kv[:part]), allowed)
            mixed = dot_rows(p.astype(LOW), kv[part:])
            v_o2[s, own, :] = gathered(mixed, wide_masks).astype(LOW)
            return carry

        lax.fori_loop(0, 4, body, 0)

    back = []
    loads[0].wait()
    loads[1].wait()
    self_part(order[0])
    own_core[0].wait_recv()
    own_core[1].wait_recv()
    first(0)
    self_part(order[1])
    first(1)
    first(2)
    second(0)
    first(3)
    second(1)
    first(4)
    third(0)
    second(2)
    third(1)
    second(3)
    arrived(0)
    arrived(1)
    self_part(order[2])
    third(2)
    second(4)
    self_part(order[3])
    third(3)
    third(4)
    back.append(copies.move(v_q1, q1))
    back.append(copies.move(v_kv1, kv1))
    back.append(copies.move(v_o1, o1))
    back.append(copies.move(v_x1, x1))
    normed(v_x1, g["ln2g"], g["ln2b"])
    for k in range(2, 5):
        loads[k].wait()
        own_core[k].wait_recv()
        arrived(k)
    for s in order:
        queries(s)
        turn(s)
    back.append(copies.move(v_turned, kv_turned))
    for i, k in enumerate((0, 1, 2, 4)):
        back.append(copies.move(v_w[k], w_back[i]))
    back.append(copies.move(v_q2, q2))
    start_sum(v_x2, v_x1, g["cob"])
    image_load.wait()
    for caption in range(captions):
        for made in images_in[caption]:
            made.wait_recv()
        cross_part(caption)
    back.append(copies.move(v_img, img))
    back.append(copies.move(v_kv2, kv2))
    back.append(copies.move(v_o2, o2))
    for s in range(4):
        v_x2[...] += dot(v_o2[s], v_w[4][s])
    back.append(copies.move(v_x2, x2))
    copies.drain()
    for made in back:
        made.wait()


def forward(dims, counts, vec, tokens, image, weights):
    captions, length, images, width, part = dims
    rows = captions * length
    shape = jax.ShapeDtypeStruct
    kept = [
        ((4, rows, part), LOW),
        ((4, 2 * part, rows), LOW),
        ((4, rows, part), LOW),
        ((rows, width), HIGH),
        ((4, rows, part), LOW),
        ((4, 2 * part, captions * images), LOW),
        ((4, rows, part), LOW),
        ((rows, width), HIGH),
        ((captions, 4, part, images), LOW),
    ]
    sizes = [(4, *w.shape) for w in weights]
    any_spec = pl.BlockSpec(memory_space=pl.ANY)
    vmem, smem = pl.BlockSpec(memory_space=pltpu.VMEM), pl.BlockSpec(memory_space=pltpu.SMEM)
    remote = 5 * 11 + 3 * captions
    return pl.pallas_call(
        partial(forward_kernel, dims),
        out_shape=[shape(*k) for k in kept]
        + [
            [shape(sizes[k], LOW) for k in (0, 1, 2, 4)],
            shape((width, 8 * part), LOW),
        ],
        in_specs=[smem] + [vmem] * 6 + [any_spec] * 7,
        out_specs=[any_spec] * 9 + [[any_spec] * 4] + [any_spec],
        scratch_shapes=[
            [pltpu.VMEM(*k) for k in kept],
            [pltpu.VMEM(sizes[k], LOW) for k in range(5)],
            pltpu.VMEM((width, 8 * part), LOW),
            pltpu.VMEM((rows, width), LOW),
            pltpu.VMEM((rows, width), LOW),
            pltpu.SemaphoreType.DMA((remote,)),
            pltpu.SemaphoreType.DMA((remote,)),
            pltpu.SemaphoreType.DMA((32,)),
        ],
        name="forward",
        compiler_params=pltpu.CompilerParams(
            collective_id=0, has_side_effects=True, vmem_limit_bytes=62 << 20
        ),
    )(counts, *vec, tokens, image, *weights)


def backward_kernel(dims, stride, *refs):
    captions, length, images, width, part = dims
    rows = captions * length
    block, wide = width // 8, width // 2
    heads = part // HEAD_SIZE
    window = 2 * length
    (
        counts,
        vec,
        (bias, tokens, grads, raw_in, raw_out),
        (q1, kv1, o1, x1, q2, kv2, o2, x2, img),
        w_back,
        kv_turned,
        sums,
        image_out,
        out_all,
        token_all,
        small_out,
        (v_q1, v_kv1, v_o1, v_x1, v_q2, v_kv2, v_o2, v_x2, v_img),
        (v_w0, v_w1, v_w2, v_w4),
        v_turned,
        (v_in, v_out, g_out, g_in, g_cross, g_self),
        v_bias,
        v_tokens,
        v_grads,
        v_h3,
        v_h,
        v_turn_a,
        v_turn_b,
        v_f0,
        v_f1,
        v_y,
        v_g,
        v_low,
        v_parts,
        v_narrow,
        from_core,
        halves,
        from_y,
        result,
        v_sum,
        sum_in,
        credit,
        send,
        recv,
        local,
    ) = refs
    d, t = lax.axis_index("dp"), lax.axis_index("tensor")
    y, c = t // 2, lax.rem(t, 2)
    near = peers()
    bits = [lax.rem(d // (stride << b), 2) for b in range(3)]
    partner = [(flipped(d, stride << b), t) for b in range(3)]
    order = [3 - t, flipped(t, 2), flipped(t, 1), t]
    copies = Copies(send, recv, local)

    mine = pl.ds(t * rows, rows)
    load_x2 = copies.move(x2, v_x2)
    load_grads = [
        copies.move(grads.at[mine], v_grads.at[0]),
        copies.move(grads.at[pl.ds(flipped(t, 2) * rows, rows)], v_grads.at[1]),
    ]
    load_mlp = [copies.move(raw_in, v_in.at[c]), copies.move(raw_out, v_out.at[c])]
    load_rest = [
        copies.move(a, b)
        for a, b in (
            (w_back[3], v_w4),
            (q2, v_q2),
            (kv2, v_kv2),
            (o2, v_o2),
            (x1, v_x1),
            (img, v_img),
            (w_back[2], v_w2),
            (kv_turned, v_turned),
            (w_back[1], v_w1),
            (w_back[0], v_w0),
            (q1, v_q1),
            (kv1, v_kv1),
            (o1, v_o1),
            (tokens.at[mine], v_tokens),
        )
    ]
    greet([*near.values(), *partner])
    mlp_in = [
        copies.to(raw_in, v_in.at[c], near["core"]),
        copies.to(raw_out, v_out.at[c], near["core"]),
        copies.to(bias, v_bias, near["core"]),
    ]

    g = as_rows(BACKWARD_VEC, vec)
    slab = 32

    def loop(body, init, step=slab):
        def run(i, carry):
            return body(pl.ds(pl.multiple_of(i * step, step), step), carry)

        return lax.fori_loop(0, rows // step, run, init)

    zeros = jnp.zeros((8, width), HIGH)

    def keep(name, total):
        v_sum[0, name : name + 1, :] = jnp.sum(total, axis=0, keepdims=True)

    pieces = [g_out, g_in, g_cross, g_self]
    plan = {
        (0, 0): (0, 1, 2),
        (0, 1): (1, 0, 2),
        (1, 0): (0, 1, 2),
        (1, 1): (1, 0, 2),
        (2, 0): ("y", 0, 1, 2),
        (2, 1): (0, 1, 2, "y"),
        (3, 0): (0, 1, 2, "y"),
        (3, 1): (1, 0, 2, "y"),
    }
    units = [(p, o, h) for p in range(4) for o in ((1,) if p < 2 else (0, 1)) for h in (0, 1)]
    y_places = {(2, 0): from_y[0], (2, 1): from_y[1], (3, 0): from_y[2], (3, 1): from_y[3]}
    to_core, hops, places = {}, {}, {}
    side = (1 - y, y)

    def lanes(h):
        return pl.ds(h * wide, wide)

    def slot(p, o):
        return p if p < 2 else 2 + o if p == 2 else o

    def own(p, o, core):
        return (core,) if p < 2 else (side[o], core)

    def offer(p, o):
        if p == 3:
            pl.semaphore_wait(credit.at[o], 1)
        to_core[p, o] = copies.to(
            pieces[p].at[own(p, o, 1 - c)], from_core.at[slot(p, o)], near["core"]
        )

    def add(target, left, *others):
        lead = left.shape[:-2]
        total = 1
        for size in lead:
            total *= size
        low = len(others) == 1 and target.dtype == LOW

        def body(i, carry):
            index, rest = [], i
            for size in reversed(lead):
                index.insert(0, lax.rem(rest, size))
                rest = rest // size
            place = (*index, slice(None), slice(None))
            value = left[place] if low else left[place].astype(HIGH)
            for ref in others:
                value = value + (ref[place] if low else ref[place].astype(HIGH))
            target[place] = value.astype(target.dtype)
            return carry

        if total == 1:
            body(0, 0)
        else:
            lax.fori_loop(0, total, body, 0)

    def cut(bit, left, value):
        return tuple(value if b == bit else slice(None) for b in sorted(left, reverse=True))

    back = []

    def advance(p, o, h, stage):
        u = units.index((p, o, h))
        turn = plan[p, h]
        y_first, with_y = turn[0] == "y", "y" in turn
        xyz = [b for b in turn if b != "y"]
        if stage == 0:
            base = pieces[p].at[(*own(p, o, c), *[slice(None)] * 4, lanes(h))]
            sent = from_core.at[(slot(p, o), *[slice(None)] * 4, lanes(h))]
            if (p, o, "core") not in places:
                to_core[p, o].wait_recv()
                places[p, o, "core"] = True
            if y_first and o == 1:
                hops[p, 0, h, "y"].wait_recv()
                add(base, base, sent, y_places[p, h])
            else:
                add(base, base, sent)
            places[u] = base, [0, 1, 2]
            if y_first and o == 0:
                hops[p, 0, h, "y"] = copies.to(base, y_places[p, h], near["y"])
                return
        if stage > 0:
            source, left = places[u]
            bit = xyz[stage - 1]
            hops[p, o, h, stage].wait_recv()
            target = halves[stage - 1].at[u]
            kept = source.at[cut(bit, left, bits[bit])]
            remaining = [b for b in left if b != bit]
            last = stage == 3
            if last and o == 1:
                total = result.at[p, :, lanes(h)]
                if y_first or not with_y:
                    add(total, target, kept)
                else:
                    hops[p, 0, h, "y"].wait_recv()
                    add(total, target, kept, y_places[p, h])
                back.append(copies.move(total, sums[p].at[:, lanes(h)]))
                return
            add(target, target, kept)
            places[u] = target, remaining
            if last:
                hops[p, 0, h, "y"] = copies.to(target, y_places[p, h], near["y"])
                return
        source, left = places[u]
        bit = xyz[stage]
        hops[p, o, h, stage + 1] = copies.to(
            source.at[cut(bit, left, 1 - bits[bit])], halves[stage].at[u], partner[bit]
        )

    def free(o):
        pl.semaphore_signal(credit.at[o], inc=1, device_id=near["core"], device_id_type=MESH)

    def forth(p, o, stage):
        advance(p, o, 0, stage)
        advance(p, o, 1, stage)

    load_x2.wait()
    for load in load_grads:
        load.wait()

    def start(place, carry):
        n, _ = norm_parts(v_x2[place, :])
        v_h3[0, place, :] = (n * g["ln3g"] + g["ln3b"]).astype(LOW)
        return carry + folded(v_grads[0, place, :].astype(HIGH))

    keep(8, loop(start, zeros))
    rows_in = copies.to(v_h3.at[0], v_h3.at[1], near["y"])
    own_rows, other_rows = slice(0, rows), slice(rows, 2 * rows)
    v_turn_a[:, own_rows] = v_h3[0].T
    v_turn_b[:, own_rows] = v_grads[0].T
    v_turn_b[:, other_rows] = v_grads[1].T

    def weight(ref, e):
        return ref[e].reshape(width, width)

    def put(ref, index, first, values):
        half, values = values
        ref[(*index, half, slice(None), slice(None), slice(None), slice(first, first + values.shape[1]))] = (
            values.astype(LOW).reshape(2, 2, block, values.shape[1])
        )

    def half_rows(half):
        return pl.ds(half * (width // 2), width // 2)

    bias_sums = [zeros, zeros]
    hidden = g_self.reshape(4 * width, width)

    def hidden_rows(kind, i, r, size=rows):
        return hidden.at[pl.ds(((kind * 2 + i) * 2 + r) * rows, size)]

    def feed(i, r):
        e = 1 - c if i else c
        v_f0[...] = dot(v_h3[r], weight(v_in, e))
        v_f1[...] = dot_rows(v_grads[r], weight(v_out, e))
        shift = (v_bias if i else bias)[...].reshape(1, -1)

        v_u, v_ga = hidden_rows(0, i, r), hidden_rows(1, i, r)

        def act(place, carry):
            a = v_f0[place, :] + shift
            cumulative = 0.5 * (1.0 + lax.erf(a * (0.5**0.5)))
            density = jnp.exp(-0.5 * a * a) * 0.3989422804014327
            v_u[place, :] = (a * cumulative).astype(LOW)
            ga = (v_f1[place, :] * (cumulative + a * density)).astype(LOW)
            v_ga[place, :] = ga
            return carry + folded(ga.astype(HIGH))

        bias_sums[i] += loop(act, zeros, 16)
        if i == 0:
            v_y[r] = dot(v_u[...], weight(v_out, e))
            v_g[r] = dot_rows(v_ga[...], weight(v_in, e))
        else:
            v_y[r] += dot(v_u[...], weight(v_out, e))
            v_g[r] += dot_rows(v_ga[...], weight(v_in, e))

    for load in load_mlp:
        load.wait()
    feed(0, 0)
    for made in mlp_in:
        made.wait_recv()
    feed(1, 0)
    rows_in.wait_recv()
    feed(0, 1)
    feed(1, 1)

    def rounded(place, carry):
        v_low[0, place, :] = v_g[1, place, :].astype(LOW)
        v_low[1, place, :] = v_y[1, place, :].astype(LOW)
        return carry

    loop(rounded, 0)
    parts_in = [copies.to(v_low.at[i], v_parts.at[i], near["y"]) for i in range(2)]
    v_turn_a[:, other_rows] = v_h3[1].T
    for i in (1, 0):
        e = 1 - c if i else c
        u, ga = (hidden_rows(kind, i, 0, size=2 * rows)[...] for kind in (0, 1))
        for half in range(2):
            put(g_out, (e,), 0, (half, dot(v_turn_b[half_rows(half), :], u)))
            put(g_in, (e,), 0, (half, dot(v_turn_a[half_rows(half), :], ga)))
        if i == 1:
            offer(0, 1)
            offer(1, 1)
    for s in range(4):
        total = jnp.sum(jnp.where(c == s % 2, bias_sums[0], bias_sums[1]), axis=0, keepdims=True)
        v_sum[0, 9 + s : 10 + s, :] = jnp.where(y == s // 2, total, 0.0)
    v_sum[0, 13:16, :] = jnp.zeros((3, width), HIGH)
    for p in (0, 1):
        forth(p, 1, 0)
        free(p)

    def shared(source, target):
        place = target.at[pl.ds(t * rows, rows)]
        back.append(copies.move(source, place))
        return [copies.to(source, place, near[name]) for name in ("core", "y", "far")]

    def norm_back(source, gain, old, new, low, more=None):
        def body(place, carry):
            a, b, e = carry
            n, inv_std = norm_parts(source[place, :].astype(HIGH))
            gh = v_g[0, place, :]
            if more is not None:
                gh = gh + more[place, :].astype(HIGH)
            scaled = gh * gain
            grad = inv_std * (
                scaled
                - jnp.mean(scaled, axis=-1, keepdims=True)
                - n * jnp.mean(scaled * n, axis=-1, keepdims=True)
            )
            grad = old[place, :].astype(HIGH) + grad
            if new is not None:
                new[place, :] = grad
                e = e + folded(grad)
            low[place, :] = grad.astype(LOW)
            return a + folded(gh * n), b + folded(gh), e

        return loop(body, (zeros, zeros, zeros))

    def finish(place, carry):
        total = v_x2[place, :] + g["mob"] + v_y[0, place, :] + v_parts[1, place, :].astype(HIGH)
        v_low[2, place, :] = total.astype(LOW)
        return carry

    for made in parts_in:
        made.wait_recv()
    loop(finish, 0)
    out_moves = shared(v_low.at[2], out_all)
    own_grads = v_grads.at[0]
    gain_sum, bias_sum, total = norm_back(
        v_x2, g["ln3g"], own_grads, v_f0, own_grads, v_parts.at[0]
    )
    keep(6, gain_sum)
    keep(7, bias_sum)
    keep(5, total)

    for load in load_rest:
        load.wait()

    def again(source, gain, shift):
        def body(place, carry):
            n, _ = norm_parts(source[place, :].astype(HIGH))
            v_h[place, :] = (n * gain + shift).astype(LOW)
            v_g[0, place, :] = jnp.zeros((slab, width), HIGH)
            return carry

        loop(body, 0)

    again(v_x1, g["ln2g"], g["ln2b"])
    v_turn_a[:, own_rows] = v_h[...].T
    v_turn_b[:, own_rows] = v_grads[0].T
    go, gq = v_narrow.at[0], v_narrow.at[1]
    masks, wide_masks = head_masks(part, LOW), head_masks(part, HIGH)

    def attend_back(q, k, v, g_mix, allowed):
        q, g_mix = spread(q, masks), spread(g_mix, masks)
        p = softmax(dot(q, k), allowed)
        low_p = p.astype(LOW)
        gp = dot(g_mix, v)
        inner = jnp.sum(gp * p, axis=-1, keepdims=True)
        gs = (p * (gp - inner)).astype(LOW)
        return (
            (gathered(dot_rows(gs, k), wide_masks) * SCALING).astype(LOW),
            (dot_columns(q, gs) * SCALING).astype(LOW),
            dot_columns(g_mix, low_p).astype(LOW),
        )

    def gradients(piece, s, of_keys, o_kept):
        for half in range(2):
            index = (s // 2, lax.rem(s, 2))
            put(piece, index, 0, (half, of_keys(half)))
            both = [dot(v_turn_a[half_rows(half), own_rows], gq[...])]
            both.append(dot(v_turn_b[half_rows(half), own_rows], o_kept[s]))
            put(piece, index, 2 * part, (half, jnp.concatenate(both, axis=1)))

    def cross_back(s):
        go[...] = dot_rows(v_grads[0], v_w4[s]).astype(LOW)

        def body(caption, carry):
            span = pl.ds(pl.multiple_of(caption * images, images), images)
            own = pl.ds(pl.multiple_of(caption * length, length), length)
            allowed = (
                lax.broadcasted_iota(jnp.int32, (1, images), 1) < counts[t * captions + caption]
            )
            g_q, g_k, g_v = attend_back(
                v_q2[s, own, :], v_kv2[s, :part, span], v_kv2[s, part:, span], go[own, :], allowed
            )
            v_kv2[s, :part, span] = g_k
            v_kv2[s, part:, span] = g_v
            gq[own, :] = g_q
            return carry

        lax.fori_loop(0, captions, body, 0)
        v_g[0] += dot(gq[...], v_w2[s])

        def of_keys(half):
            total = 0
            for caption in range(captions):
                span = slice(caption * images, (caption + 1) * images)
                features = v_img[caption, 2 * half : 2 * half + 2].reshape(width // 2, images)
                total = total + dot_rows(features, v_kv2[s, :, span])
            return total

        gradients(g_cross, s, of_keys, v_o2)

    for i, s in enumerate(order):
        cross_back(s)
        if i == 0:
            offer(2, 0)
            forth(0, 1, 1)
        if i == 1:
            forth(1, 1, 1)
            forth(2, 0, 0)
        if i == 2:
            offer(2, 1)
            forth(0, 1, 2)
        if i == 3:
            forth(1, 1, 2)
            advance(2, 0, 1, 1)
            advance(2, 1, 1, 0)
    image_span = pl.ds(t * captions, captions)

    def image_part(caption, carry):
        span = pl.ds(pl.multiple_of(caption * images, images), images)
        values = dot(v_turned[...], v_kv2[:, :, span].reshape(8 * part, images))
        v_img[caption] = values.astype(LOW).reshape(4, part, images)
        return carry

    lax.fori_loop(0, captions, image_part, 0)
    forth(0, 1, 3)
    image_moves = [
        copies.to(v_img.at[:, target], image_out.at[image_span], near[name])
        for name, target in (("y", flipped(t, 2)), ("far", 3 - t), ("core", flipped(t, 1)))
    ]
    back.append(copies.move(v_img.at[:, t], image_out.at[image_span]))
    gain_sum, bias_sum, total = norm_back(v_x1, g["ln2g"], v_f0, v_f1, own_grads)
    keep(3, gain_sum)
    keep(4, bias_sum)
    keep(2, total)
    forth(1, 1, 3)
    advance(2, 1, 0, 0)
    advance(2, 0, 1, 2)

    again(v_tokens, g["ln1g"], g["ln1b"])
    v_turn_a[:, own_rows] = v_h[...].T
    v_turn_b[:, own_rows] = v_grads[0].T
    causal = window_allowed(length, window, heads)

    def self_back(s):
        go[...] = dot_rows(v_grads[0], v_w1[s]).astype(LOW)
        for w in range(rows // window):
            span = pl.ds(w * window, window)
            g_q, g_k, g_v = attend_back(
                v_q1[s, span, :], v_kv1[s, :part, span], v_kv1[s, part:, span], go[span, :], causal
            )
            v_kv1[s, :part, span] = g_k
            v_kv1[s, part:, span] = g_v
            gq[span, :] = g_q
        v_g[0] += dot(gq[...], v_w0[s, :part, :]) + dot_columns(v_kv1[s], v_w0[s, part:, :])

        def of_keys(half):
            return dot_rows(v_turn_a[half_rows(half), own_rows], v_kv1[s])

        gradients(g_self, s, of_keys, v_o1)

    for i, s in enumerate(order):
        self_back(s)
        if i == 0:
            offer(3, 0)
            advance(2, 1, 1, 1)
            advance(2, 1, 0, 1)
            advance(2, 0, 1, 3)
        if i == 1:
            forth(3, 0, 0)
            advance(2, 1, 1, 2)
        if i == 2:
            offer(3, 1)
            advance(2, 1, 0, 2)
        if i == 3:
            forth(3, 0, 1)
            forth(2, 1, 3)
    forth(3, 1, 0)
    gain_sum, bias_sum, _ = norm_back(v_tokens, g["ln1g"], v_f1, None, v_h)
    keep(0, gain_sum)
    keep(1, bias_sum)
    small_to = [near["core"], *partner, near["y"]]
    small = []

    def total_start():
        i = len(small)
        small.append(copies.to(v_sum.at[i], sum_in.at[i], small_to[i]))

    def total_end():
        i = len(small) - 1
        small[i].wait_recv()
        v_sum[i + 1] = v_sum[i] + sum_in[i]

    total_start()
    token_moves = shared(v_h, token_all)
    forth(3, 0, 2)
    total_end()
    total_start()
    forth(3, 1, 1)
    total_end()
    total_start()
    forth(3, 0, 3)
    total_end()
    total_start()
    forth(3, 1, 2)
    total_end()
    total_start()
    forth(3, 1, 3)
    total_end()
    back.append(copies.move(v_sum.at[5], small_out))
    for made in out_moves + image_moves + token_moves:
        made.wait_recv()
    copies.drain()
    for made in back:
        made.wait()


def backward(dims, stride, counts, vec, bias, tokens, grads, raw, kept, w_back, turned):
    captions, length, images, width, part = dims
    rows = captions * length
    block, wide = width // 8, width // 2
    shape = jax.ShapeDtypeStruct
    any_spec = pl.BlockSpec(memory_space=pl.ANY)
    vmem, smem = pl.BlockSpec(memory_space=pltpu.VMEM), pl.BlockSpec(memory_space=pltpu.SMEM)
    shard = (2, 2, 2, block, width)
    raw = [w.reshape(shard) for w in raw]
    remote = 128

    def scratch(*size, dtype=LOW):
        return pltpu.VMEM(size, dtype)

    flat = [scratch(*k.shape, dtype=k.dtype) for k in kept]
    return pl.pallas_call(
        lambda *refs: backward_kernel(
            dims,
            stride,
            refs[0],
            refs[1:8],
            refs[8:13],
            refs[13:22],
            refs[22:26],
            refs[26],
            refs[27:31],
            *refs[31:],
        ),
        out_shape=[shape((block, width), HIGH)] * 4
        + [
            shape((4 * captions, part, images), LOW),
            shape((4 * rows, width), LOW),
            shape((4 * rows, width), LOW),
            shape((16, width), HIGH),
        ],
        in_specs=[smem] + [vmem] * 8 + [any_spec] * 18,
        out_specs=[any_spec] * 8,
        scratch_shapes=[
            flat,
            [scratch(*w.shape) for w in w_back],
            scratch(*turned.shape),
            [scratch(2, *shard)] * 4 + [scratch(2, 2, *shard)] * 2,
            scratch(*bias.shape, dtype=HIGH),
            scratch(rows, width),
            scratch(2, rows, width),
            scratch(2, rows, width),
            scratch(rows, width),
            scratch(width, 2 * rows),
            scratch(width, 2 * rows),
            scratch(rows, width, dtype=HIGH),
            scratch(rows, width, dtype=HIGH),
            scratch(2, rows, width, dtype=HIGH),
            scratch(2, rows, width, dtype=HIGH),
            scratch(3, rows, width),
            scratch(2, rows, width),
            scratch(2, rows, part),
            scratch(4, *shard),
            [
                scratch(12, 2, 2, block, wide),
                scratch(12, 2, block, wide),
                scratch(12, block, wide),
            ],
            [scratch(2, 2, 2, block, wide)] + [scratch(block, wide)] * 3,
            scratch(4, block, width, dtype=HIGH),
            scratch(6, 16, width, dtype=HIGH),
            scratch(5, 16, width, dtype=HIGH),
            pltpu.SemaphoreType.REGULAR((2,)),
            pltpu.SemaphoreType.DMA((remote,)),
            pltpu.SemaphoreType.DMA((remote,)),
            pltpu.SemaphoreType.DMA((48,)),
        ],
        name="backward",
        compiler_params=pltpu.CompilerParams(
            collective_id=1, has_side_effects=True, vmem_limit_bytes=67043328
        ),
    )(counts, *vec, bias, tokens, grads, *raw, *kept, *w_back, turned)


def local(
    tokens,
    image_tokens,
    image_counts,
    ln1_gain,
    ln1_bias,
    self_qkv,
    self_output_weight,
    self_output_bias,
    ln2_gain,
    ln2_bias,
    cross_query_weight,
    cross_kv,
    cross_output_weight,
    cross_output_bias,
    ln3_gain,
    ln3_bias,
    mlp_in,
    mlp_in_bias,
    mlp_out,
    mlp_out_bias,
    grad_out,
):
    stride = lax.axis_size("dp") // 8
    all_captions, length, width = tokens.shape
    images, part = image_tokens.shape[1:]
    captions = all_captions // 4
    dims = (captions, length, images, width, part)
    first = [ln1_gain, ln1_bias, self_output_bias, ln2_gain, ln2_bias, cross_output_bias]
    second = [ln1_gain, ln1_bias, ln2_gain, ln2_bias, ln3_gain, ln3_bias, mlp_out_bias]
    tokens = tokens.reshape(-1, width)
    grads = grad_out.reshape(-1, width)
    weights = [
        self_qkv.transpose(1, 2, 0).reshape(3 * part, width),
        self_output_weight,
        cross_query_weight.T,
        cross_kv.transpose(1, 2, 0).reshape(2 * part, width),
        cross_output_weight,
    ]
    *kept, w_back, turned = forward(
        dims, image_counts, first, tokens, image_tokens.transpose(0, 2, 1), weights
    )
    sum_out, sum_in, sum_cross, sum_self, grad_image, output, grad_tokens, small = backward(
        dims,
        stride,
        image_counts,
        second,
        mlp_in_bias,
        tokens,
        grads,
        (mlp_in, mlp_out),
        kept,
        w_back,
        turned,
    )
    if stride > 1:
        groups = [[hi * stride + lo for lo in range(stride)] for hi in range(8)]
        sum_out, sum_in, sum_cross, sum_self = (
            lax.psum_scatter(s, "dp", scatter_dimension=0, axis_index_groups=groups, tiled=True)
            for s in (sum_out, sum_in, sum_cross, sum_self)
        )
        small = lax.psum(small, "dp", axis_index_groups=groups)
    own_bias = lax.dynamic_index_in_dim(small, 9 + lax.axis_index("tensor"), 0, keepdims=False)
    keys, rest = slice(0, part), slice(part, 2 * part)
    third, fourth = slice(2 * part, 3 * part), slice(3 * part, 4 * part)
    return (
        output.reshape(all_captions, length, width),
        grad_tokens.reshape(all_captions, length, width),
        grad_image.transpose(0, 2, 1),
        small[0],
        small[1],
        jnp.stack([sum_self[:, third], sum_self[:, keys], sum_self[:, rest]], axis=1),
        sum_self[:, fourth].T,
        small[2],
        small[3],
        small[4],
        sum_cross[:, third],
        sum_cross[:, : 2 * part].reshape(-1, 2, part),
        sum_cross[:, fourth].T,
        small[5],
        small[6],
        small[7],
        sum_in,
        own_bias,
        sum_out.T,
        small[8],
    )


def solution(mesh):
    return jax.shard_map(
        local,
        mesh=mesh,
        in_specs=(
            P("dp", None, None),
            P("dp", None, "tensor"),
            P("dp"),
            P(),
            P(),
            P(None, None, "tensor"),
            P("tensor", None),
            P(),
            P(),
            P(),
            P(None, "tensor"),
            P(None, None, "tensor"),
            P("tensor", None),
            P(),
            P(),
            P(),
            P(None, "tensor"),
            P("tensor"),
            P("tensor", None),
            P(),
            P("dp", None, None),
        ),
        out_specs=(
            P("dp", None, None),
            P("dp", None, None),
            P("dp", None, "tensor"),
            P(),
            P(),
            P("dp", None, "tensor"),
            P("tensor", "dp"),
            P(),
            P(),
            P(),
            P("dp", "tensor"),
            P("dp", None, "tensor"),
            P("tensor", "dp"),
            P(),
            P(),
            P(),
            P("dp", "tensor"),
            P("tensor"),
            P("tensor", "dp"),
            P(),
        ),
        check_vma=False,
    )
```

time: 248 us -> 189 us (0.76)
  Pallas kernels: 226 us -> 176 us
  local copies, waits for them, and re-layouts: 20.3 us -> 11.6 us
    pallas_call x1, Pallas kernels: 152 us -> 124 us  [backward(): pl.pallas_call(lambda *refs: backward_kernel(dims, stride, refs[0], refs[...]
    pallas_call x1, Pallas kernels: 73.9 us -> 52 us  [forward(): pl.pallas_call(partial(forward_kernel, dims), out_shape=[shape(*k) for k...]
    another operation x9 -> x0, local copies, waits for them, and re-layouts: 6.2 us -> none  [local(): vec = jnp.concatenate([jnp.stack(rows), jnp.zeros((7, width), HIGH)])]
where the time goes in v2:
time: 189 us
  Pallas kernels  176 us (93%)
  local copies, waits for them, and re-layouts  11.6 us (6%)
    pallas_call x1, Pallas kernels, backward(): pl.pallas_call(lambda *refs: backward_kernel(dims, stride, refs[0], refs[...  124 us
    pallas_call x1, Pallas kernels, forward(): pl.pallas_call(partial(forward_kernel, dims), out_shape=[shape(*k) for k...  52 us
    unnamed x21, local copies, waits for them, and re-layouts  8.02 us

profile of v2, /device:TPU:0, one launch (start us, length us, event | category | flops | bytes accessed | tf_op | source)
XLA Modules:
  0.0 188.6 jit_solution(15943692010949005991)
XLA Ops:
  0.7 52.0 %forward.1 = (bf16[4,256,192]{2,1,0:T(8,128)(2,1)}, bf16[4,384,256]{2,1,0:T(8,128)(2,1)}, bf16[4,256,192]{2,1,0:T(8,128)(2,1)}, f32[256,768]{1,0:T(8,128)}, bf16...) custom-call(s32[16]{0:T(128)} %refs_0_.3, ...), custom_call_target="tpu_custom_call" | custom-call | tf_op jit(solution)/shard_map/forward/pallas_call | solution.py:347
  52.7 123.6 %backward.1 = (f32[96,768]{1,0:T(8,128)}, f32[96,768]{1,0:T(8,128)}, f32[96,768]{1,0:T(8,128)}, f32[96,768]{1,0:T(8,128)}, bf16[16,192,256]{2,1,0:T(8,128)(2,1)}...) custom-call(s32[16]{0:T(128)} %refs_0_.3, f32[768]{0:T(1024)} %refs_1_.3, f32[768]{0:T(1024)} %refs_2_.3, ...), custom_call_target="tpu_custom_call" | custom-call | tf_op jit(solution)/shard_map/backward/pallas_call | solution.py:929
  176.3 0.0 copy-start.3
  176.3 0.0 copy-start.6
  176.3 0.0 copy-start.2
  176.3 2.0 %slice_bitcast_fusion = (f32[192,96]{0,1:T(8,128)S(1)}, f32[96,192]{1,0:T(8,128)}, f32[96,1,192]{2,0,1:T(8,128)S(1)}, f32[96,1,192]{2,0,1:T(8,128)S(1)}, f32[96,1,192]{2,0,1:T(8,128)S(1)}, /*index=5*/f32[192,96]{0,1:T(8,128)S(1)}) fusion(f32[96,768]{1,0:T(8,128)} %get-tuple-element.61, f32[96,768]{1,0:T(8,128)} %get-tuple-element.60), kind=kLoop, calls=%fused_computation.1 | loop fusion | bytes 884736 | tf_op jit(solution)/shard_map/transpose | solution.py:1070
  178.3 0.7 pad_maximum_fusion
  179.0 0.7 copy.41
  179.8 0.7 copy.42
  180.5 0.0 copy-done.3
  180.5 0.9 reshape.75
  181.4 0.0 copy-done.6
  181.4 0.7 slice_reduce_fusion
  182.1 0.0 copy-done.2
  182.1 0.0 copy-start.1
  182.1 1.1 copy.48
  183.2 0.8 copy-done.1
  184.0 0.0 copy-start
  184.0 1.1 copy.49
  185.2 0.8 copy-done
  186.0 0.0 copy-start.5
  186.0 0.0 copy-start.4
  186.0 1.1 copy.50
  187.2 0.0 copy-done.5
  187.2 0.7 copy.51
  187.9 0.0 copy-done.4
  187.9 0.7 copy.52
  (1 shorter events, 0.0 us)
Async XLA Ops:
  176.3 4.3 %copy-start.3 = (f32[96,768]{1,0:T(8,128)S(1)}, f32[96,768]{1,0:T(8,128)}, u32[]{:S(2)}) copy-start(f32[96,768]{1,0:T(8,128)} %get-tuple-element.61) | copy-start | bytes 884740
  176.3 5.1 %copy-start.6 = (f32[16,768]{1,0:T(8,128)S(1)}, f32[16,768]{1,0:T(8,128)}, u32[]{:S(2)}) copy-start(f32[16,768]{1,0:T(8,128)} %get-tuple-element.59) | copy-start | bytes 147460
  176.3 5.8 %copy-start.2 = (bf16[1024,768]{1,0:T(8,128)(2,1)S(1)}, bf16[1024,768]{1,0:T(8,128)(2,1)}, u32[]{:S(2)}) copy-start(bf16[1024,768]{1,0:T(8,128)(2,1)} %get-tuple-element.56) | copy-start | bytes 4718596
  182.1 2.0 %copy-start.1 = (bf16[1024,768]{1,0:T(8,128)(2,1)S(1)}, bf16[1024,768]{1,0:T(8,128)(2,1)}, u32[]{:S(2)}) copy-start(bf16[1024,768]{1,0:T(8,128)(2,1)} %get-tuple-element.57) | copy-start | bytes 4718596
  184.0 2.0 %copy-start = (bf16[16,192,256]{2,1,0:T(8,128)(2,1)S(1)}, bf16[16,192,256]{2,1,0:T(8,128)(2,1)}, u32[]{:S(2)}) copy-start(bf16[16,192,256]{2,1,0:T(8,128)(2,1)} %get-tuple-element.58) | copy-start | bytes 4718596
  186.0 1.1 copy-start.5
  186.0 1.9 copy-start.4

commit v3 on v2

--- a/solution.py
+++ b/solution.py
@@ -113,8 +113,8 @@
     return total
 
 
-FORWARD_VEC = ("ln1g", "ln1b", "sob", "ln2g", "ln2b", "cob")
-BACKWARD_VEC = ("ln1g", "ln1b", "ln2g", "ln2b", "ln3g", "ln3b", "mob")
+FORWARD_VEC = ("ln1g", "ln1b", "sob", "ln2g", "ln2b", "cob", "ln3g", "ln3b")
+BACKWARD_VEC = ("ln1g", "ln1b", "ln2g", "ln2b", "ln3g", "mob")
 
 
 def as_rows(names, refs):
@@ -124,15 +124,17 @@
 def forward_kernel(dims, *refs):
     captions, length, images, width, part = dims
     rows = captions * length
-    (counts, *vec), refs = refs[:7], refs[7:]
-    (tokens, image, *weights), refs = refs[:7], refs[7:]
+    (counts, *vec), refs = refs[:9], refs[9:]
+    (tokens, image, raw_in, raw_out, *weights), refs = refs[:9], refs[9:]
     (q1, kv1, o1, x1, q2, kv2, o2, x2, img, w_back, kv_turned), refs = refs[:11], refs[11:]
+    (own_h3, other_h3, other_in, other_out), refs = refs[:4], refs[4:]
     (
         (v_q1, v_kv1, v_o1, v_x1, v_q2, v_kv2, v_o2, v_x2, v_img),
         v_w,
         v_turned,
         v_tokens,
         v_h,
+        v_h3,
         send,
         recv,
         local,
@@ -179,6 +181,9 @@
         ]
         for caption in range(captions)
     ]
+    mlp_in = [
+        copies.to(a, b, near["core"]) for a, b in ((raw_in, other_in), (raw_out, other_out))
+    ]
     core = {k: [] for k in range(count)}
 
     def first(k):
@@ -205,7 +210,7 @@
         for made in core[k]:
             made.wait_recv()
 
-    slab = 32
+    slab = 64
 
     def normed(source, gain, shift):
         def body(i, carry):
@@ -265,7 +270,15 @@
             return carry
 
         lax.fori_loop(0, 4, body, 0)
-
+        total = v_x2[own, :]
+        for s in range(4):
+            total = total + dot(v_o2[s, own, :], v_w[4][s])
+        v_x2[own, :] = total
+        n, _ = norm_parts(total)
+        v_h3[own, :] = (n * g["ln3g"] + g["ln3b"]).astype(LOW)
+        h3_in.append(copies.to(v_h3.at[own], other_h3.at[own], near["y"]))
+
+    h3_in = []
     back = []
     loads[0].wait()
     loads[1].wait()
@@ -317,15 +330,16 @@
     back.append(copies.move(v_img, img))
     back.append(copies.move(v_kv2, kv2))
     back.append(copies.move(v_o2, o2))
-    for s in range(4):
-        v_x2[...] += dot(v_o2[s], v_w[4][s])
     back.append(copies.move(v_x2, x2))
+    back.append(copies.move(v_h3, own_h3))
+    for made in mlp_in + h3_in:
+        made.wait_recv()
     copies.drain()
     for made in back:
         made.wait()
 
 
-def forward(dims, counts, vec, tokens, image, weights):
+def forward(dims, counts, vec, tokens, image, raw, weights):
     captions, length, images, width, part = dims
     rows = captions * length
     shape = jax.ShapeDtypeStruct
@@ -343,20 +357,25 @@
     sizes = [(4, *w.shape) for w in weights]
     any_spec = pl.BlockSpec(memory_space=pl.ANY)
     vmem, smem = pl.BlockSpec(memory_space=pltpu.VMEM), pl.BlockSpec(memory_space=pltpu.SMEM)
-    remote = 5 * 11 + 3 * captions
+    remote = 5 * 11 + 4 * captions + 2
     return pl.pallas_call(
         partial(forward_kernel, dims),
         out_shape=[shape(*k) for k in kept]
         + [
             [shape(sizes[k], LOW) for k in (0, 1, 2, 4)],
             shape((width, 8 * part), LOW),
+            shape((rows, width), LOW),
+            shape((rows, width), LOW),
+            shape(raw[0].shape, LOW),
+            shape(raw[1].shape, LOW),
         ],
-        in_specs=[smem] + [vmem] * 6 + [any_spec] * 7,
-        out_specs=[any_spec] * 9 + [[any_spec] * 4] + [any_spec],
+        in_specs=[smem] + [vmem] * 8 + [any_spec] * 9,
+        out_specs=[any_spec] * 9 + [[any_spec] * 4] + [any_spec] * 5,
         scratch_shapes=[
             [pltpu.VMEM(*k) for k in kept],
             [pltpu.VMEM(sizes[k], LOW) for k in range(5)],
             pltpu.VMEM((width, 8 * part), LOW),
+            pltpu.VMEM((rows, width), LOW),
             pltpu.VMEM((rows, width), LOW),
             pltpu.VMEM((rows, width), LOW),
             pltpu.SemaphoreType.DMA((remote,)),
@@ -367,7 +386,7 @@
         compiler_params=pltpu.CompilerParams(
             collective_id=0, has_side_effects=True, vmem_limit_bytes=62 << 20
         ),
-    )(counts, *vec, tokens, image, *weights)
+    )(counts, *vec, tokens, image, *raw, *weights)
 
 
 def backward_kernel(dims, stride, *refs):
@@ -379,7 +398,7 @@
     (
         counts,
         vec,
-        (bias, tokens, grads, raw_in, raw_out),
+        (bias, tokens, grads, raw_in, raw_out, own_h3, other_h3, other_in, other_out),
         (q1, kv1, o1, x1, q2, kv2, o2, x2, img),
         w_back,
         kv_turned,
@@ -431,7 +450,11 @@
         copies.move(grads.at[mine], v_grads.at[0]),
         copies.move(grads.at[pl.ds(flipped(t, 2) * rows, rows)], v_grads.at[1]),
     ]
-    load_mlp = [copies.move(raw_in, v_in.at[c]), copies.move(raw_out, v_out.at[c])]
+    load_mlp = [
+        [copies.move(a, v_h3.at[i]) for i, a in ((0, own_h3), (1, other_h3))],
+        [copies.move(raw_in, v_in.at[c]), copies.move(raw_out, v_out.at[c])],
+        [copies.move(other_in, v_in.at[1 - c]), copies.move(other_out, v_out.at[1 - c])],
+    ]
     load_rest = [
         copies.move(a, b)
         for a, b in (
@@ -452,14 +475,10 @@
         )
     ]
     greet([*near.values(), *partner])
-    mlp_in = [
-        copies.to(raw_in, v_in.at[c], near["core"]),
-        copies.to(raw_out, v_out.at[c], near["core"]),
-        copies.to(bias, v_bias, near["core"]),
-    ]
+    bias_in = copies.to(bias, v_bias, near["core"])
 
     g = as_rows(BACKWARD_VEC, vec)
-    slab = 32
+    slab = 64
 
     def loop(body, init, step=slab):
         def run(i, carry):
@@ -588,21 +607,7 @@
         advance(p, o, 0, stage)
         advance(p, o, 1, stage)
 
-    load_x2.wait()
-    for load in load_grads:
-        load.wait()
-
-    def start(place, carry):
-        n, _ = norm_parts(v_x2[place, :])
-        v_h3[0, place, :] = (n * g["ln3g"] + g["ln3b"]).astype(LOW)
-        return carry + folded(v_grads[0, place, :].astype(HIGH))
-
-    keep(8, loop(start, zeros))
-    rows_in = copies.to(v_h3.at[0], v_h3.at[1], near["y"])
     own_rows, other_rows = slice(0, rows), slice(rows, 2 * rows)
-    v_turn_a[:, own_rows] = v_h3[0].T
-    v_turn_b[:, own_rows] = v_grads[0].T
-    v_turn_b[:, other_rows] = v_grads[1].T
 
     def weight(ref, e):
         return ref[e].reshape(width, width)
@@ -647,14 +652,12 @@
             v_y[r] += dot(v_u[...], weight(v_out, e))
             v_g[r] += dot_rows(v_ga[...], weight(v_in, e))
 
-    for load in load_mlp:
+    for load in load_grads + load_mlp[0] + load_mlp[1]:
         load.wait()
-    feed(0, 0)
-    for made in mlp_in:
-        made.wait_recv()
-    feed(1, 0)
-    rows_in.wait_recv()
     feed(0, 1)
+    for load in load_mlp[2]:
+        load.wait()
+    bias_in.wait_recv()
     feed(1, 1)
 
     def rounded(place, carry):
@@ -664,7 +667,17 @@
 
     loop(rounded, 0)
     parts_in = [copies.to(v_low.at[i], v_parts.at[i], near["y"]) for i in range(2)]
+    feed(0, 0)
+    feed(1, 0)
+
+    def start(place, carry):
+        return carry + folded(v_grads[0, place, :].astype(HIGH))
+
+    keep(8, loop(start, zeros))
+    v_turn_a[:, own_rows] = v_h3[0].T
     v_turn_a[:, other_rows] = v_h3[1].T
+    v_turn_b[:, own_rows] = v_grads[0].T
+    v_turn_b[:, other_rows] = v_grads[1].T
     for i in (1, 0):
         e = 1 - c if i else c
         u, ga = (hidden_rows(kind, i, 0, size=2 * rows)[...] for kind in (0, 1))
@@ -685,7 +698,12 @@
     def shared(source, target):
         place = target.at[pl.ds(t * rows, rows)]
         back.append(copies.move(source, place))
-        return [copies.to(source, place, near[name]) for name in ("core", "y", "far")]
+        return [copies.to(source, place, near[name]) for name in ("y", "core")]
+
+    def passed_on(moves, target):
+        place = target.at[pl.ds(flipped(t, 2) * rows, rows)]
+        moves[0].wait_recv()
+        return [moves[1], copies.to(place, place, near["core"])]
 
     def norm_back(source, gain, old, new, low, more=None):
         def body(place, carry):
@@ -714,10 +732,8 @@
         v_low[2, place, :] = total.astype(LOW)
         return carry
 
-    for made in parts_in:
-        made.wait_recv()
-    loop(finish, 0)
-    out_moves = shared(v_low.at[2], out_all)
+    load_x2.wait()
+    parts_in[0].wait_recv()
     own_grads = v_grads.at[0]
     gain_sum, bias_sum, total = norm_back(
         v_x2, g["ln3g"], own_grads, v_f0, own_grads, v_parts.at[0]
@@ -798,6 +814,9 @@
     for i, s in enumerate(order):
         cross_back(s)
         if i == 0:
+            parts_in[1].wait_recv()
+            loop(finish, 0)
+            out_moves = shared(v_low.at[2], out_all)
             offer(2, 0)
             forth(0, 1, 1)
         if i == 1:
@@ -806,6 +825,7 @@
         if i == 2:
             offer(2, 1)
             forth(0, 1, 2)
+            out_moves = passed_on(out_moves, out_all)
         if i == 3:
             forth(1, 1, 2)
             advance(2, 0, 1, 1)
@@ -868,9 +888,6 @@
         if i == 2:
             offer(3, 1)
             advance(2, 1, 0, 2)
-        if i == 3:
-            forth(3, 0, 1)
-            forth(2, 1, 3)
     forth(3, 1, 0)
     gain_sum, bias_sum, _ = norm_back(v_tokens, g["ln1g"], v_f1, None, v_h)
     keep(0, gain_sum)
@@ -889,18 +906,21 @@
 
     total_start()
     token_moves = shared(v_h, token_all)
-    forth(3, 0, 2)
+    forth(3, 0, 1)
+    forth(2, 1, 3)
     total_end()
     total_start()
     forth(3, 1, 1)
     total_end()
     total_start()
+    forth(3, 0, 2)
+    total_end()
+    total_start()
+    forth(3, 1, 2)
     forth(3, 0, 3)
     total_end()
     total_start()
-    forth(3, 1, 2)
-    total_end()
-    total_start()
+    token_moves = passed_on(token_moves, token_all)
     forth(3, 1, 3)
     total_end()
     back.append(copies.move(v_sum.at[5], small_out))
@@ -911,7 +931,7 @@
         made.wait()
 
 
-def backward(dims, stride, counts, vec, bias, tokens, grads, raw, kept, w_back, turned):
+def backward(dims, stride, counts, vec, bias, tokens, grads, raw, mlp, kept, w_back, turned):
     captions, length, images, width, part = dims
     rows = captions * length
     block, wide = width // 8, width // 2
@@ -920,6 +940,8 @@
     vmem, smem = pl.BlockSpec(memory_space=pltpu.VMEM), pl.BlockSpec(memory_space=pltpu.SMEM)
     shard = (2, 2, 2, block, width)
     raw = [w.reshape(shard) for w in raw]
+    own_h3, other_h3, *others = mlp
+    mlp = [own_h3, other_h3, *(w.reshape(shard) for w in others)]
     remote = 128
 
     def scratch(*size, dtype=LOW):
@@ -931,13 +953,13 @@
             dims,
             stride,
             refs[0],
-            refs[1:8],
-            refs[8:13],
-            refs[13:22],
-            refs[22:26],
-            refs[26],
-            refs[27:31],
-            *refs[31:],
+            refs[1:7],
+            refs[7:16],
+            refs[16:25],
+            refs[25:29],
+            refs[29],
+            refs[30:34],
+            *refs[34:],
         ),
         out_shape=[shape((block, width), HIGH)] * 4
         + [
@@ -946,7 +968,7 @@
             shape((4 * rows, width), LOW),
             shape((16, width), HIGH),
         ],
-        in_specs=[smem] + [vmem] * 8 + [any_spec] * 18,
+        in_specs=[smem] + [vmem] * 7 + [any_spec] * 22,
         out_specs=[any_spec] * 8,
         scratch_shapes=[
             flat,
@@ -986,7 +1008,78 @@
         compiler_params=pltpu.CompilerParams(
             collective_id=1, has_side_effects=True, vmem_limit_bytes=67043328
         ),
-    )(counts, *vec, bias, tokens, grads, *raw, *kept, *w_back, turned)
+    )(counts, *vec, bias, tokens, grads, *raw, *mlp, *kept, *w_back, turned)
+
+
+def finish_kernel(dims, *refs):
+    captions, length, images, width, part = dims
+    ins, refs = refs[:8], refs[8:]
+    outs, vectors, refs = (*refs[:9], refs[19]), refs[9:19], refs[20:]
+    buffers, made_qkv, made_self, made_q, made_cross, made_kv, arrive, leave = refs
+    loads = [
+        pltpu.make_async_copy(a, b, arrive.at[i]) for i, (a, b) in enumerate(zip(ins, buffers))
+    ]
+    for load in loads[::-1]:
+        load.start()
+    v_self, v_cross, v_small = buffers[:3]
+    leaving = []
+
+    def put(source, target):
+        made = pltpu.make_async_copy(source, target, leave.at[len(leaving)])
+        made.start()
+        leaving.append(made)
+
+    def columns(ref, i):
+        return ref[:, i * part : (i + 1) * part]
+
+    for i in range(7, 2, -1):
+        loads[i].wait()
+        put(buffers[i], outs[i + 1])
+    loads[0].wait()
+    for i, j in enumerate((2, 0, 1)):
+        made_qkv[i] = columns(v_self, j)
+    put(made_qkv, outs[0])
+    made_self[...] = columns(v_self, 3).T
+    put(made_self, outs[1])
+    loads[1].wait()
+    made_q[...] = columns(v_cross, 2)
+    put(made_q, outs[2])
+    made_cross[...] = columns(v_cross, 3).T
+    put(made_cross, outs[3])
+    for i in range(2):
+        made_kv[:, i, :] = columns(v_cross, i)
+    put(made_kv, outs[9])
+    loads[2].wait()
+    for i, ref in enumerate(vectors[:9]):
+        ref[...] = v_small[i : i + 1, :].reshape(width)
+    own = v_small[pl.ds(9 + lax.axis_index("tensor"), 1), :]
+    vectors[9][...] = own.reshape(width)
+    for made in leaving:
+        made.wait()
+
+
+def finish(dims, ins):
+    captions, length, images, width, part = dims
+    block = ins[0].shape[0]
+    any_spec, vmem = pl.BlockSpec(memory_space=pl.ANY), pl.BlockSpec(memory_space=pltpu.VMEM)
+    made = [(3, block, part), (part, block), (block, part), (part, block)]
+    return pl.pallas_call(
+        partial(finish_kernel, dims),
+        out_shape=[jax.ShapeDtypeStruct(size, HIGH) for size in made]
+        + [jax.ShapeDtypeStruct(x.shape, x.dtype) for x in ins[3:]]
+        + [jax.ShapeDtypeStruct((width,), HIGH)] * 10
+        + [jax.ShapeDtypeStruct((block, 2, part), HIGH)],
+        in_specs=[any_spec] * 8,
+        out_specs=[any_spec] * 9 + [vmem] * 10 + [any_spec],
+        scratch_shapes=[
+            [pltpu.VMEM(x.shape, x.dtype) for x in ins],
+            *(pltpu.VMEM(size, HIGH) for size in made),
+            pltpu.VMEM((block, 2, part), HIGH),
+            pltpu.SemaphoreType.DMA((8,)),
+            pltpu.SemaphoreType.DMA((10,)),
+        ],
+        name="finish",
+    )(*ins)
 
 
 def local(
@@ -1018,7 +1111,8 @@
     captions = all_captions // 4
     dims = (captions, length, images, width, part)
     first = [ln1_gain, ln1_bias, self_output_bias, ln2_gain, ln2_bias, cross_output_bias]
-    second = [ln1_gain, ln1_bias, ln2_gain, ln2_bias, ln3_gain, ln3_bias, mlp_out_bias]
+    first += [ln3_gain, ln3_bias]
+    second = [ln1_gain, ln1_bias, ln2_gain, ln2_bias, ln3_gain, mlp_out_bias]
     tokens = tokens.reshape(-1, width)
     grads = grad_out.reshape(-1, width)
     weights = [
@@ -1028,8 +1122,9 @@
         cross_kv.transpose(1, 2, 0).reshape(2 * part, width),
         cross_output_weight,
     ]
-    *kept, w_back, turned = forward(
-        dims, image_counts, first, tokens, image_tokens.transpose(0, 2, 1), weights
+    raw = (mlp_in, mlp_out)
+    *kept, w_back, turned, own_h3, other_h3, other_in, other_out = forward(
+        dims, image_counts, first, tokens, image_tokens.transpose(0, 2, 1), raw, weights
     )
     sum_out, sum_in, sum_cross, sum_self, grad_image, output, grad_tokens, small = backward(
         dims,
@@ -1039,7 +1134,8 @@
         mlp_in_bias,
         tokens,
         grads,
-        (mlp_in, mlp_out),
+        raw,
+        (own_h3, other_h3, other_in, other_out),
         kept,
         w_back,
         turned,
@@ -1051,30 +1147,31 @@
             for s in (sum_out, sum_in, sum_cross, sum_self)
         )
         small = lax.psum(small, "dp", axis_index_groups=groups)
-    own_bias = lax.dynamic_index_in_dim(small, 9 + lax.axis_index("tensor"), 0, keepdims=False)
-    keys, rest = slice(0, part), slice(part, 2 * part)
-    third, fourth = slice(2 * part, 3 * part), slice(3 * part, 4 * part)
+    qkv, self_out, cross_q, cross_out, sum_in, sum_out, *rest = finish(
+        dims, [sum_self, sum_cross, small, sum_in, sum_out, output, grad_tokens, grad_image]
+    )
+    output, grad_tokens, grad_image, *vectors, cross_kv = rest
     return (
         output.reshape(all_captions, length, width),
         grad_tokens.reshape(all_captions, length, width),
         grad_image.transpose(0, 2, 1),
-        small[0],
-        small[1],
-        jnp.stack([sum_self[:, third], sum_self[:, keys], sum_self[:, rest]], axis=1),
-        sum_self[:, fourth].T,
-        small[2],
-        small[3],
-        small[4],
-        sum_cross[:, third],
-        sum_cross[:, : 2 * part].reshape(-1, 2, part),
-        sum_cross[:, fourth].T,
-        small[5],
-        small[6],
-        small[7],
+        vectors[0],
+        vectors[1],
+        qkv.transpose(1, 0, 2),
+        self_out,
+        vectors[2],
+        vectors[3],
+        vectors[4],
+        cross_q,
+        cross_kv,
+        cross_out,
+        vectors[5],
+        vectors[6],
+        vectors[7],
         sum_in,
-        own_bias,
+        vectors[9],
         sum_out.T,
-        small[8],
+        vectors[8],
     )
 
 

time: 189 us -> 169 us (0.89)
  local copies, waits for them, and re-layouts: 11.6 us -> 0 us
  Pallas kernels: 176 us -> 168 us
    pallas_call x1, Pallas kernels: 124 us -> 106 us  [backward(): pl.pallas_call(lambda *refs: backward_kernel(dims, stride, refs[0], refs[...]
    unnamed x21 -> x0, local copies, waits for them, and re-layouts: 8.02 us -> none
    pallas_call x0 -> x1, Pallas kernels: none -> 5.49 us  [finish(): pl.pallas_call(partial(finish_kernel, dims), out_shape=[jax.ShapeDtypeStr...]
    pallas_call x1, Pallas kernels: 52 us -> 56.8 us  [forward(): pl.pallas_call(partial(forward_kernel, dims), out_shape=[shape(*k) for k...]
    transpose x1 -> x0, local copies, waits for them, and re-layouts: 2.01 us -> none  [local(): sum_cross[:, fourth]]
where the time goes in v3:
time: 169 us
  Pallas kernels  168 us (99%)
    pallas_call x1, Pallas kernels, backward(): pl.pallas_call(lambda *refs: backward_kernel(dims, stride, refs[0], refs[...  106 us
    pallas_call x1, Pallas kernels, forward(): pl.pallas_call(partial(forward_kernel, dims), out_shape=[shape(*k) for k...  56.8 us
    pallas_call x1, Pallas kernels, finish(): pl.pallas_call(partial(finish_kernel, dims), out_shape=[jax.ShapeDtypeStr...  5.49 us

profile of v3, /device:TPU:0, one launch (start us, length us, event | category | flops | bytes accessed | tf_op | source)
XLA Modules:
  0.0 169.2 jit_solution(15709759365408754632)
XLA Ops:
  0.7 56.8 %forward.1 = (bf16[4,256,192]{2,1,0:T(8,128)(2,1)}, bf16[4,384,256]{2,1,0:T(8,128)(2,1)}, bf16[4,256,192]{2,1,0:T(8,128)(2,1)}, f32[256,768]{1,0:T(8,128)}, bf16...) custom-call(s32[16]{0:T(128)} %refs_0_.3, ...), custom_call_target="tpu_custom_call" | custom-call | tf_op jit(solution)/shard_map/forward/pallas_call | solution.py:361
  57.5 106.1 %backward.1 = (f32[96,768]{1,0:T(8,128)}, f32[96,768]{1,0:T(8,128)}, f32[96,768]{1,0:T(8,128)}, f32[96,768]{1,0:T(8,128)}, bf16[16,192,256]{2,1,0:T(8,128)(2,1)}...) custom-call(s32[16]{0:T(128)} %refs_0_.3, f32[768]{0:T(1024)} %refs_1_.3, f32[768]{0:T(1024)} %refs_2_.3, ...), custom_call_target="tpu_custom_call" | custom-call | tf_op jit(solution)/shard_map/backward/pallas_call | solution.py:951
  163.6 5.5 %finish.1 = (f32[3,96,192]{2,1,0:T(8,128)}, f32[192,96]{1,0:T(8,128)}, f32[96,192]{1,0:T(8,128)}, f32[192,96]{1,0:T(8,128)}, f32[96,768]{1,0:T(8,128)}, /*index=...) custom-call(f32[96,768]{1,0:T(8,128)} %get-tuple-element.84.refs_0_,, ...), custom_call_target="tpu_custom_call" | custom-call | tf_op jit(solution)/shard_map/finish/pallas_call | solution.py:1066

commit v4 on v3

--- a/solution.py
+++ b/solution.py
@@ -181,9 +181,6 @@
         ]
         for caption in range(captions)
     ]
-    mlp_in = [
-        copies.to(a, b, near["core"]) for a, b in ((raw_in, other_in), (raw_out, other_out))
-    ]
     core = {k: [] for k in range(count)}
 
     def first(k):
@@ -250,26 +247,56 @@
             v_o1[s, span, :] = gathered(mixed, wide_masks).astype(LOW)
         v_x1[...] += dot(v_o1[s], v_w[1][s])
 
-    def queries(s):
-        v_q2[s] = dot_rows(v_h[...], v_w[2][s]).astype(LOW)
-
-    def turn(s):
-        v_turned[:, pl.ds(pl.multiple_of(s * 2 * part, 128), 2 * part)] = v_w[3][s].T
+    def queries(groups):
+        def body(i, carry):
+            s = pair(groups, i)
+            v_q2[s] = dot_rows(v_h[...], v_w[2][s]).astype(LOW)
+            return carry
+
+        lax.fori_loop(0, 2, body, 0)
+
+    def turn(groups):
+        def body(i, carry):
+            s = pair(groups, i)
+            v_turned[:, pl.ds(pl.multiple_of(s * 2 * part, 128), 2 * part)] = v_w[3][s].T
+            return carry
+
+        lax.fori_loop(0, 2, body, 0)
+
+    def spans(c):
+        return (
+            pl.ds(pl.multiple_of(c * images, images), images),
+            pl.ds(pl.multiple_of(c * length, length), length),
+        )
+
+    def pair(groups, i):
+        return groups[0] + i * (groups[1] - groups[0])
+
+    def mix(c, s):
+        allowed = lax.broadcasted_iota(jnp.int32, (1, images), 1) < counts[t * captions + c]
+        span, own = spans(c)
+        kv = dot(v_w[3][s], v_img[c].reshape(width, images)).astype(LOW)
+        v_kv2[s, :, span] = kv
+        q = spread(v_q2[s, own, :], masks)
+        p = softmax(dot(q, kv[:part]), allowed)
+        mixed = dot_rows(p.astype(LOW), kv[part:])
+        v_o2[s, own, :] = gathered(mixed, wide_masks).astype(LOW)
+
+    def near_part(first_caption, count):
+        def body(i, carry):
+            mix(first_caption + i // 2, pair(order[:2], lax.rem(i, 2)))
+            return carry
+
+        lax.fori_loop(0, 2 * count, body, 0)
 
     def cross_part(c):
-        allowed = lax.broadcasted_iota(jnp.int32, (1, images), 1) < counts[t * captions + c]
-        span, own = pl.ds(c * images, images), pl.ds(c * length, length)
-
-        def body(s, carry):
-            kv = dot(v_w[3][s], v_img[c].reshape(width, images)).astype(LOW)
-            v_kv2[s, :, span] = kv
-            q = spread(v_q2[s, own, :], masks)
-            p = softmax(dot(q, kv[:part]), allowed)
-            mixed = dot_rows(p.astype(LOW), kv[part:])
-            v_o2[s, own, :] = gathered(mixed, wide_masks).astype(LOW)
+        own = spans(c)[1]
+
+        def body(i, carry):
+            mix(c, pair(order[2:], i))
             return carry
 
-        lax.fori_loop(0, 4, body, 0)
+        lax.fori_loop(0, 2, body, 0)
         total = v_x2[own, :]
         for s in range(4):
             total = total + dot(v_o2[s, own, :], v_w[4][s])
@@ -280,6 +307,11 @@
 
     h3_in = []
     back = []
+
+    def image_arrived(c):
+        for made in images_in[c]:
+            made.wait_recv()
+
     loads[0].wait()
     loads[1].wait()
     self_part(order[0])
@@ -288,45 +320,58 @@
     first(0)
     self_part(order[1])
     first(1)
+    for k in range(2, 5):
+        loads[k].wait()
+        own_core[k].wait_recv()
+    turn(order[:2])
+    second(0)
+    second(1)
     first(2)
-    second(0)
     first(3)
-    second(1)
     first(4)
     third(0)
-    second(2)
     third(1)
-    second(3)
+    image_load.wait()
     arrived(0)
     arrived(1)
-    self_part(order[2])
+    second(2)
+
+    def far_self(i, carry):
+        self_part(pair(order[2:], i))
+        return carry
+
+    lax.fori_loop(0, 2, far_self, 0)
+    second(3)
+    second(4)
+    normed(v_x1, g["ln2g"], g["ln2b"])
+    queries(order[:2])
+    start_sum(v_x2, v_x1, g["cob"])
+    image_arrived(0)
+    image_arrived(1)
+    near_part(0, 2)
     third(2)
-    second(4)
-    self_part(order[3])
     third(3)
     third(4)
+    mlp_in = [
+        copies.to(a, b, near["core"]) for a, b in ((raw_in, other_in), (raw_out, other_out))
+    ]
     back.append(copies.move(v_q1, q1))
     back.append(copies.move(v_kv1, kv1))
     back.append(copies.move(v_o1, o1))
     back.append(copies.move(v_x1, x1))
-    normed(v_x1, g["ln2g"], g["ln2b"])
+    for caption in range(2, captions):
+        image_arrived(caption)
+    near_part(2, captions - 2)
     for k in range(2, 5):
-        loads[k].wait()
-        own_core[k].wait_recv()
         arrived(k)
-    for s in order:
-        queries(s)
-        turn(s)
-    back.append(copies.move(v_turned, kv_turned))
     for i, k in enumerate((0, 1, 2, 4)):
         back.append(copies.move(v_w[k], w_back[i]))
+    queries(order[2:])
     back.append(copies.move(v_q2, q2))
-    start_sum(v_x2, v_x1, g["cob"])
-    image_load.wait()
     for caption in range(captions):
-        for made in images_in[caption]:
-            made.wait_recv()
         cross_part(caption)
+    turn(order[2:])
+    back.append(copies.move(v_turned, kv_turned))
     back.append(copies.move(v_img, img))
     back.append(copies.move(v_kv2, kv2))
     back.append(copies.move(v_o2, o2))
@@ -497,8 +542,8 @@
         (0, 1): (1, 0, 2),
         (1, 0): (0, 1, 2),
         (1, 1): (1, 0, 2),
-        (2, 0): ("y", 0, 1, 2),
-        (2, 1): (0, 1, 2, "y"),
+        (2, 0): ("y", 1, 0, 2),
+        (2, 1): (1, 0, 2, "y"),
         (3, 0): (0, 1, 2, "y"),
         (3, 1): (1, 0, 2, "y"),
     }
@@ -820,15 +865,13 @@
             offer(2, 0)
             forth(0, 1, 1)
         if i == 1:
-            forth(1, 1, 1)
             forth(2, 0, 0)
         if i == 2:
             offer(2, 1)
-            forth(0, 1, 2)
+            forth(1, 1, 1)
             out_moves = passed_on(out_moves, out_all)
         if i == 3:
-            forth(1, 1, 2)
-            advance(2, 0, 1, 1)
+            forth(0, 1, 2)
             advance(2, 1, 1, 0)
     image_span = pl.ds(t * captions, captions)
 
@@ -839,7 +882,8 @@
         return carry
 
     lax.fori_loop(0, captions, image_part, 0)
-    forth(0, 1, 3)
+    forth(1, 1, 2)
+    advance(2, 0, 1, 1)
     image_moves = [
         copies.to(v_img.at[:, target], image_out.at[image_span], near[name])
         for name, target in (("y", flipped(t, 2)), ("far", 3 - t), ("core", flipped(t, 1)))
@@ -849,9 +893,8 @@
     keep(3, gain_sum)
     keep(4, bias_sum)
     keep(2, total)
-    forth(1, 1, 3)
+    forth(0, 1, 3)
     advance(2, 1, 0, 0)
-    advance(2, 0, 1, 2)
 
     again(v_tokens, g["ln1g"], g["ln1b"])
     v_turn_a[:, own_rows] = v_h[...].T
@@ -879,15 +922,16 @@
         self_back(s)
         if i == 0:
             offer(3, 0)
+            forth(1, 1, 3)
             advance(2, 1, 1, 1)
-            advance(2, 1, 0, 1)
-            advance(2, 0, 1, 3)
+            advance(2, 0, 1, 2)
         if i == 1:
             forth(3, 0, 0)
-            advance(2, 1, 1, 2)
+            advance(2, 1, 0, 1)
         if i == 2:
             offer(3, 1)
-            advance(2, 1, 0, 2)
+            advance(2, 1, 1, 2)
+            advance(2, 0, 1, 3)
     forth(3, 1, 0)
     gain_sum, bias_sum, _ = norm_back(v_tokens, g["ln1g"], v_f1, None, v_h)
     keep(0, gain_sum)
@@ -906,6 +950,7 @@
 
     total_start()
     token_moves = shared(v_h, token_all)
+    advance(2, 1, 0, 2)
     forth(3, 0, 1)
     forth(2, 1, 3)
     total_end()

time: 169 us -> 166 us (0.982)
  Pallas kernels: 168 us -> 165 us
    pallas_call x1, Pallas kernels: 56.8 us -> 53.4 us  [forward(): pl.pallas_call(partial(forward_kernel, dims), out_shape=[shape(*k) for k...]
where the time goes in v4:
time: 166 us; the launch traced here: 165 us
  Pallas kernels  165 us (99%)
    pallas_call x1, Pallas kernels, backward(): pl.pallas_call(lambda *refs: backward_kernel(dims, stride, refs[0], refs[...  106 us
    pallas_call x1, Pallas kernels, forward(): pl.pallas_call(partial(forward_kernel, dims), out_shape=[shape(*k) for k...  53.4 us
    pallas_call x1, Pallas kernels, finish(): pl.pallas_call(partial(finish_kernel, dims), out_shape=[jax.ShapeDtypeStr...  5.49 us

profile of v4, /device:TPU:0, one launch (start us, length us, event | category | flops | bytes accessed | tf_op | source)
XLA Modules:
  0.0 165.4 jit_solution(3625894500303441983)
XLA Ops:
  0.7 53.4 %forward.1 = (bf16[4,256,192]{2,1,0:T(8,128)(2,1)}, bf16[4,384,256]{2,1,0:T(8,128)(2,1)}, bf16[4,256,192]{2,1,0:T(8,128)(2,1)}, f32[256,768]{1,0:T(8,128)}, bf16...) custom-call(s32[16]{0:T(128)} %refs_0_.3, ...), custom_call_target="tpu_custom_call" | custom-call | tf_op jit(solution)/shard_map/forward/pallas_call | solution.py:406
  54.1 105.6 %backward.1 = (f32[96,768]{1,0:T(8,128)}, f32[96,768]{1,0:T(8,128)}, f32[96,768]{1,0:T(8,128)}, f32[96,768]{1,0:T(8,128)}, bf16[16,192,256]{2,1,0:T(8,128)(2,1)}...) custom-call(s32[16]{0:T(128)} %refs_0_.3, f32[768]{0:T(1024)} %refs_1_.3, f32[768]{0:T(1024)} %refs_2_.3, ...), custom_call_target="tpu_custom_call" | custom-call | tf_op jit(solution)/shard_map/backward/pallas_call | solution.py:996
  159.7 5.5 %finish.1 = (f32[3,96,192]{2,1,0:T(8,128)}, f32[192,96]{1,0:T(8,128)}, f32[96,192]{1,0:T(8,128)}, f32[192,96]{1,0:T(8,128)}, f32[96,768]{1,0:T(8,128)}, /*index=...) custom-call(f32[96,768]{1,0:T(8,128)} %get-tuple-element.84.refs_0_,, ...), custom_call_target="tpu_custom_call" | custom-call | tf_op jit(solution)/shard_map/finish/pallas_call | solution.py:1111
